TPU v7x, 128 devices: a whole 4x4x4 slice. The times are simulated.
128 devices in a mesh: gx: 8 (over z, x_hi), gy: 4 (over y), gz: 4 (over x_lo, core).
Axes of the slice: x: 4 (x_hi: 2, x_lo: 2; x = x_hi * 2 + x_lo), y: 4, z: 4, core: 2. Of those that a mesh axis runs over, the one named last changes fastest.
Arguments:
- state: float32 [53, 32, 16, 512], P(None, 'gx', 'gy', 'gz'), may hold values from -8 to 8
- diffusivity: float32 [53], replicated, may hold values from 0.01 to 0.08
- rates: float32 [53, 53], replicated, may hold values from -1.75 to 1.75
- inverse: float32 [53, 53, 32, 16, 512], P(None, None, 'gx', 'gy', 'gz'), may hold values from -3 to 5
- boundary: int32 [3], replicated, may hold values from 0 to 1, as said below
Outputs:
- new_state: float32 [53, 32, 16, 512], P(None, 'gx', 'gy', 'gz')
Inputs may be any that keep to these rules, and one draw needn't show every extreme that they name: `boundary`: 1 marks a dimension with periodic faces, 0 one with mirrored walls; at least one dimension has each kind.
All inputs are finite; a program needn't handle non-finite values.
Results may differ from a plain program's by a relative error of at most 0.00014.
Values sent between devices are 32-bit elements; how exact they have to be, the bound alone decides.
A program may use at most 128 MiB of HBM per device.

v0:
```python
import jax
import jax.numpy as jnp
from jax import lax
from jax.sharding import PartitionSpec as P

NEWTON = 2


implicit_gamma = 0.2928932188134524
explicit_delta = -0.7071067811865475
rel_tol = 0.1
abs_tol = 0.05
drift_speed = 0.2


def with_halo(array, sides, width):
    edges = {}
    for axis, dim in sides:
        size, length = (lax.axis_size(axis), array.shape[dim])
        up = [(i, (i + 1) % size) for i in range(size)]
        last = lax.slice_in_dim(array, length - width, length, axis=dim)
        leading = lax.slice_in_dim(array, 0, width, axis=dim)
        edges[dim] = (
            lax.ppermute(last, axis, up),
            lax.ppermute(leading, axis, [(b, a) for a, b in up]),
        )
    done = []
    for _, dim in sides:
        low, high = edges[dim]
        around = [(width, width) if d in done else (0, 0) for d in range(array.ndim)]
        array = jnp.concatenate([jnp.pad(low, around), array, jnp.pad(high, around)], axis=dim)
        done.append(dim)
    return array


def from_everyone(array, axis):
    copies = jnp.broadcast_to(array, (lax.axis_size(axis), *array.shape))
    return lax.all_to_all(copies, axis, split_axis=0, concat_axis=0, tiled=True)


def of_everyone(array, axis):
    everything = from_everyone(array, axis)
    return jnp.sum(everything, axis=0)


def mirror_walls(extended, dim, flag, position, last_index):
    length = extended.shape[dim]
    low_ghost = lax.slice_in_dim(extended, 0, 2, axis=dim)
    high_ghost = lax.slice_in_dim(extended, length - 2, length, axis=dim)
    low_edge = jnp.flip(lax.slice_in_dim(extended, 2, 4, axis=dim), dim)
    high_edge = jnp.flip(lax.slice_in_dim(extended, length - 4, length - 2, axis=dim), dim)
    middle = lax.slice_in_dim(extended, 2, length - 2, axis=dim)
    walled = flag == 0
    low_part = jnp.where(walled & (position == 0), low_edge, low_ghost)
    high_part = jnp.where(walled & (position == last_index), high_edge, high_ghost)
    return jnp.concatenate([low_part, middle, high_part], axis=dim)


def stencil_terms(extended, dim):
    length = extended.shape[dim] - 4
    parts = [lax.slice_in_dim(extended, k, k + length, axis=dim) for k in range(5)]
    second = (-parts[0] + 16.0 * parts[1] - 30.0 * parts[2] + 16.0 * parts[3] - parts[4]) / 12.0
    return (second, parts[1])


def axis_terms(extended, dim, flag, axis_name):
    if axis_name == "gx":
        fixed = mirror_walls(extended, dim, flag, lax.axis_index("gx"), lax.axis_size("gx") - 1)
    elif axis_name == "gy":
        fixed = mirror_walls(extended, dim, flag, lax.axis_index("gy"), lax.axis_size("gy") - 1)
    else:
        fixed = mirror_walls(extended, dim, flag, lax.axis_index("gz"), lax.axis_size("gz") - 1)
    return stencil_terms(fixed, dim)


def transport(field, diffusivity, boundary):
    padded = with_halo(field, (("gx", 1), ("gy", 2), ("gz", 3)), 2)
    lap_x, below_x = axis_terms(padded[:, :, 2:-2, 2:-2], 1, boundary[0], "gx")
    lap_y, unused_y = axis_terms(padded[:, 2:-2, :, 2:-2], 2, boundary[1], "gy")
    lap_z, unused_z = axis_terms(padded[:, 2:-2, 2:-2, :], 3, boundary[2], "gz")
    return diffusivity[:, None, None, None] * (lap_x + lap_y + lap_z) - drift_speed * (
        field - below_x
    )


def chemistry(field, rates):
    return jnp.einsum("sj,jxyz->sxyz", rates, jnp.tanh(field), precision=lax.Precision.HIGHEST)


def global_total(local):
    partial_z = of_everyone(local, "gz")
    partial_y = of_everyone(partial_z, "gy")
    return of_everyone(partial_y, "gx")


def newton_solve(base, inverse, rates, weights):
    entries = base.shape[0] * base.shape[1] * base.shape[2] * base.shape[3]
    entries = entries * lax.axis_size("gx") * lax.axis_size("gy") * lax.axis_size("gz")
    guess = base
    for sweep in range(NEWTON):
        residual = guess - base - implicit_gamma * chemistry(guess, rates)
        update = jnp.einsum("sjxyz,jxyz->sxyz", inverse, residual, precision=lax.Precision.HIGHEST)
        local = jnp.sum(jnp.square(update * weights))
        norm_value = jnp.sqrt(global_total(local) / float(entries))
        guess = guess - update / jnp.maximum(norm_value, 1.0)
    return guess


def body(state, diffusivity, rates, inverse, boundary):
    weights = 1.0 / (rel_tol * jnp.abs(state) + abs_tol)
    first_rate = transport(state, diffusivity, boundary)
    section = newton_solve(state + implicit_gamma * first_rate, inverse, rates, weights)
    second_rate = transport(section, diffusivity, boundary)
    base = state + explicit_delta * first_rate + (1.0 - explicit_delta) * second_rate
    base = base + (1.0 - implicit_gamma) * chemistry(section, rates)
    return newton_solve(base, inverse, rates, weights)


def solution(mesh):
    in_specs = (P(None, "gx", "gy", "gz"), P(), P(), P(None, None, "gx", "gy", "gz"), P())
    out_specs = P(None, "gx", "gy", "gz")
    return jax.shard_map(body, mesh=mesh, in_specs=in_specs, out_specs=out_specs, check_vma=False)
```

profile of v0, /device:TPU:1, one launch (start us, length us, event | category | flops | bytes accessed | tf_op | source)
XLA Modules:
  0.0 227.5 jit_solution(3669746642263484878)
XLA Ops:
  4.2 6.2 %collective-permute-start.1 = (f32[53,2,4,128]{3,0,2,1:T(8,128)S(1)}, f32[53,2,4,128]{3,0,2,1:T(8,128)}, u32[]{:S(2)}, u32[]{:S(2)}) collective-permute-start(f32[53,2,4,128]{3,0,2,1:T(8,128)S(1)} %get-tuple-element.14), channel_id=1, source_target_pairs={{16,0},{32,16},{48,32},{64,48},{80,64},{96,80},{112,96},{0,112},{1... | collective-permute-start | bytes 651272 | tf_op jit(solution)/shard_map/ppermute | solution.py:25
  20.4 2.2 collective-permute-done.1
  23.6 7.2 %collective-permute-done = f32[53,2,4,128]{3,0,2,1:T(8,128)} collective-permute-done((f32[53,2,4,128]{3,0,2,1:T(8,128)S(1)}, f32[53,2,4,128]{3,0,2,1:T(8,128)}, u32[]{:S(2)}, u32[]{:S(2)}) %collective-permute-start) | collective-permute-done | bytes 217120 | tf_op jit(solution)/shard_map/ppermute | solution.py:24
  33.7 2.0 fusion.13
  35.9 10.1 %multiply_reduce_fusion.3 = f32[4,4,128,53]{2,1,0,3:T(4,128)S(1)} fusion(f32[53,53,4,4,128]{4,3,2,1,0:T(4,128)} %param.8, f32[4,4,128,53]{2,1,0,3:T(4,128)S(1)} %copy.117), kind=kLoop, calls=%fused_computation.3 | loop fusion | flops 11397120 | bytes 23879680
  47.5 5.8 %all_to_all.72 = f32[4,1,1]{2,1,0:T(1,128)S(1)} all-to-all(f32[4,1,1]{2,1,0:T(1,128)S(1)} %broadcast_in_dim.38), channel_id=1, replica_groups=mesh['gx'=8,'gy'=4,'gz'=4] {'gz'}, dimensions={0} | all-to-all | bytes 32 | tf_op jit(solution)/shard_map/all_to_all | solution.py:38
  54.6 8.2 %all_to_all.73 = f32[4,1,1]{2,1,0:T(1,128)S(1)} all-to-all(f32[4,1,1]{2,1,0:T(1,128)S(1)} %broadcast_in_dim.39), channel_id=1, replica_groups=mesh['gx'=8,'gy'=4,'gz'=4] {'gy'}, dimensions={0} | all-to-all | bytes 32 | tf_op jit(solution)/shard_map/all_to_all | solution.py:38
  64.1 8.9 %all_to_all.74 = f32[8,1,1]{2,1,0:T(1,128)S(1)} all-to-all(f32[8,1,1]{2,1,0:T(1,128)S(1)} %broadcast_in_dim.40), channel_id=1, replica_groups=mesh['gx'=8,'gy'=4,'gz'=4] {'gx'}, dimensions={0} | all-to-all | bytes 64 | tf_op jit(solution)/shard_map/all_to_all | solution.py:38
  75.5 10.1 %multiply_reduce_fusion.2 = f32[4,4,128,53]{2,1,0,3:T(4,128)S(1)} fusion(f32[53,53,4,4,128]{4,3,2,1,0:T(4,128)} %param.8, f32[4,4,128,53]{2,1,0,3:T(4,128)S(1)} %copy.118), kind=kLoop, calls=%fused_computation.2 | loop fusion | flops 11397120 | bytes 23879680
  87.1 8.7 %all_to_all.75 = f32[4,1,1]{2,1,0:T(1,128)S(1)} all-to-all(f32[4,1,1]{2,1,0:T(1,128)S(1)} %broadcast_in_dim.41), channel_id=1, replica_groups=mesh['gx'=8,'gy'=4,'gz'=4] {'gz'}, dimensions={0} | all-to-all | bytes 32 | tf_op jit(solution)/shard_map/all_to_all | solution.py:38
  97.1 6.5 %all_to_all.76 = f32[4,1,1]{2,1,0:T(1,128)S(1)} all-to-all(f32[4,1,1]{2,1,0:T(1,128)S(1)} %broadcast_in_dim.42), channel_id=1, replica_groups=mesh['gx'=8,'gy'=4,'gz'=4] {'gy'}, dimensions={0} | all-to-all | bytes 32 | tf_op jit(solution)/shard_map/all_to_all | solution.py:38
  104.8 8.9 %all_to_all.77 = f32[8,1,1]{2,1,0:T(1,128)S(1)} all-to-all(f32[8,1,1]{2,1,0:T(1,128)S(1)} %broadcast_in_dim.43), channel_id=1, replica_groups=mesh['gx'=8,'gy'=4,'gz'=4] {'gx'}, dimensions={0} | all-to-all | bytes 64 | tf_op jit(solution)/shard_map/all_to_all | solution.py:38
  116.5 2.6 %collective-permute-start.10 = (f32[53,4,4,2]{3,0,2,1:T(8,128)S(1)}, f32[53,4,4,2]{3,0,2,1:T(8,128)}, u32[]{:S(2)}, u32[]{:S(2)}) collective-permute-start(f32[53,4,4,2]{3,0,2,1:T(8,128)S(1)} %get-tuple-element.6), channel_id=1, source_target_pairs={{0,1},{1,2},{2,3},{3,0},{4,5},{5,6},{6,7},{7,4},{8,9},{9,10},{10,1... | collective-permute-start | bytes 20360 | tf_op jit(solution)/shard_map/ppermute | solution.py:24
  121.1 4.5 %collective-permute-start.7 = (f32[53,2,4,128]{3,0,2,1:T(8,128)}, f32[53,2,4,128]{3,0,2,1:T(8,128)S(1)}, u32[]{:S(2)}, u32[]{:S(2)}) collective-permute-start(f32[53,2,4,128]{3,0,2,1:T(8,128)} %get-tuple-element.8), channel_id=1, source_target_pairs={{16,0},{32,16},{48,32},{64,48},{80,64},{96,80},{112,96},{0,112},{1... | collective-permute-start | bytes 651272 | tf_op jit(solution)/shard_map/ppermute | solution.py:25
  129.5 3.4 %collective-permute-done.11 = f32[53,4,4,2]{3,0,2,1:T(8,128)} collective-permute-done((f32[53,4,4,2]{3,0,2,1:T(8,128)S(1)}, f32[53,4,4,2]{3,0,2,1:T(8,128)}, u32[]{:S(2)}, u32[]{:S(2)}) %collective-permute-start.11) | collective-permute-done | bytes 6816 | tf_op jit(solution)/shard_map/ppermute | solution.py:25
  135.1 3.3 %collective-permute-done.7 = f32[53,2,4,128]{3,0,2,1:T(8,128)S(1)} collective-permute-done((f32[53,2,4,128]{3,0,2,1:T(8,128)}, f32[53,2,4,128]{3,0,2,1:T(8,128)S(1)}, u32[]{:S(2)}, u32[]{:S(2)}) %collective-permute-start.7) | collective-permute-done | bytes 217120 | tf_op jit(solution)/shard_map/ppermute | solution.py:25
  142.6 10.1 %multiply_reduce_fusion.1 = f32[4,4,128,53]{2,1,0,3:T(4,128)S(1)} fusion(f32[53,53,4,4,128]{4,3,2,1,0:T(4,128)} %param.8, f32[4,4,128,53]{2,1,0,3:T(4,128)S(1)} %copy.119), kind=kLoop, calls=%fused_computation.1 | loop fusion | flops 11397120 | bytes 23879680
  154.2 8.2 %all_to_all.78 = f32[4,1,1]{2,1,0:T(1,128)S(1)} all-to-all(f32[4,1,1]{2,1,0:T(1,128)S(1)} %broadcast_in_dim.44), channel_id=1, replica_groups=mesh['gx'=8,'gy'=4,'gz'=4] {'gz'}, dimensions={0} | all-to-all | bytes 32 | tf_op jit(solution)/shard_map/all_to_all | solution.py:38
  163.7 6.5 %all_to_all.79 = f32[4,1,1]{2,1,0:T(1,128)S(1)} all-to-all(f32[4,1,1]{2,1,0:T(1,128)S(1)} %broadcast_in_dim.45), channel_id=1, replica_groups=mesh['gx'=8,'gy'=4,'gz'=4] {'gy'}, dimensions={0} | all-to-all | bytes 32 | tf_op jit(solution)/shard_map/all_to_all | solution.py:38
  171.5 13.1 %all_to_all.80 = f32[8,1,1]{2,1,0:T(1,128)S(1)} all-to-all(f32[8,1,1]{2,1,0:T(1,128)S(1)} %broadcast_in_dim.46), channel_id=1, replica_groups=mesh['gx'=8,'gy'=4,'gz'=4] {'gx'}, dimensions={0} | all-to-all | bytes 64 | tf_op jit(solution)/shard_map/all_to_all | solution.py:38
  186.8 10.1 %multiply_reduce_fusion = f32[4,4,128,53]{2,1,0,3:T(4,128)S(1)} fusion(f32[53,53,4,4,128]{4,3,2,1,0:T(4,128)} %param.8, f32[4,4,128,53]{2,1,0,3:T(4,128)S(1)} %copy.120), kind=kLoop, calls=%fused_computation | loop fusion | flops 11397120 | bytes 23879680
  198.5 8.7 %all_to_all.81 = f32[4,1,1]{2,1,0:T(1,128)S(1)} all-to-all(f32[4,1,1]{2,1,0:T(1,128)S(1)} %broadcast_in_dim.47), channel_id=1, replica_groups=mesh['gx'=8,'gy'=4,'gz'=4] {'gz'}, dimensions={0} | all-to-all | bytes 32 | tf_op jit(solution)/shard_map/all_to_all | solution.py:38
  208.4 6.5 %all_to_all.82 = f32[4,1,1]{2,1,0:T(1,128)S(1)} all-to-all(f32[4,1,1]{2,1,0:T(1,128)S(1)} %broadcast_in_dim.48), channel_id=1, replica_groups=mesh['gx'=8,'gy'=4,'gz'=4] {'gy'}, dimensions={0} | all-to-all | bytes 32 | tf_op jit(solution)/shard_map/all_to_all | solution.py:38
  216.2 8.9 %all_to_all.83 = f32[8,1,1]{2,1,0:T(1,128)S(1)} all-to-all(f32[8,1,1]{2,1,0:T(1,128)S(1)} %broadcast_in_dim.49), channel_id=1, replica_groups=mesh['gx'=8,'gy'=4,'gz'=4] {'gx'}, dimensions={0} | all-to-all | bytes 64 | tf_op jit(solution)/shard_map/all_to_all | solution.py:38
  (86 shorter events, 51.9 us)
Async XLA Ops:
  0.0 33.7 %copy-start = (f32[53,53]{1,0:T(8,128)S(1)}, f32[53,53]{1,0:T(8,128)}, u32[]{:S(2)}) copy-start(f32[53,53]{1,0:T(8,128)} %param.7) | copy-start | bytes 33712
  0.0 45.9 %copy-start.1 = (f32[53,4,4,128]{3,2,1,0:T(4,128)S(1)}, f32[53,4,4,128]{3,2,1,0:T(4,128)}, u32[]{:S(2)}) copy-start(f32[53,4,4,128]{3,2,1,0:T(4,128)} %param.5) | copy-start | bytes 1302532
  1.4 15.2 %collective-permute-start.5 = (f32[53,4,4,2]{3,0,2,1:T(8,128)S(1)}, f32[53,4,4,2]{3,0,2,1:T(8,128)}, u32[]{:S(2)}, u32[]{:S(2)}) collective-permute-start(f32[53,4,4,2]{3,0,2,1:T(8,128)S(1)} %get-tuple-element.11), channel_id=1, source_target_pairs={{1,0},{2,1},{3,2},{0,3},{5,4},{6,5},{7,6},{4,7},{9,8},{10,9},{11,1... | collective-permute-start | bytes 20360 | tf_op jit(solution)/shard_map/ppermute | solution.py:25
  2.9 16.4 %collective-permute-start.4 = (f32[53,4,4,2]{3,0,2,1:T(8,128)S(1)}, f32[53,4,4,2]{3,0,2,1:T(8,128)}, u32[]{:S(2)}, u32[]{:S(2)}) collective-permute-start(f32[53,4,4,2]{3,0,2,1:T(8,128)S(1)} %get-tuple-element.12), channel_id=1, source_target_pairs={{0,1},{1,2},{2,3},{3,0},{4,5},{5,6},{6,7},{7,4},{8,9},{9,10},{10,1... | collective-permute-start | bytes 20360 | tf_op jit(solution)/shard_map/ppermute | solution.py:24
  4.2 18.4 %collective-permute-start.1 = (f32[53,2,4,128]{3,0,2,1:T(8,128)S(1)}, f32[53,2,4,128]{3,0,2,1:T(8,128)}, u32[]{:S(2)}, u32[]{:S(2)}) collective-permute-start(f32[53,2,4,128]{3,0,2,1:T(8,128)S(1)} %get-tuple-element.14), channel_id=1, source_target_pairs={{16,0},{32,16},{48,32},{64,48},{80,64},{96,80},{112,96},{0,112},{1... | collective-permute-start | bytes 651272 | tf_op jit(solution)/shard_map/ppermute | solution.py:25
  10.4 20.4 %collective-permute-start = (f32[53,2,4,128]{3,0,2,1:T(8,128)S(1)}, f32[53,2,4,128]{3,0,2,1:T(8,128)}, u32[]{:S(2)}, u32[]{:S(2)}) collective-permute-start(f32[53,2,4,128]{3,0,2,1:T(8,128)S(1)} %get-tuple-element.13), channel_id=1, source_target_pairs={{0,16},{16,32},{32,48},{48,64},{64,80},{80,96},{96,112},{112,0},{1... | collective-permute-start | bytes 651272 | tf_op jit(solution)/shard_map/ppermute | solution.py:24
  11.1 20.7 %collective-permute-start.2 = (f32[53,4,2,128]{3,0,2,1:T(8,128)S(1)}, f32[53,4,2,128]{3,0,2,1:T(8,128)}, u32[]{:S(2)}, u32[]{:S(2)}) collective-permute-start(f32[53,4,2,128]{3,0,2,1:T(8,128)S(1)} %get-tuple-element.15), channel_id=1, source_target_pairs={{0,4},{4,8},{8,12},{12,0},{1,5},{5,9},{9,13},{13,1},{2,6},{6,10},{... | collective-permute-start | bytes 651272 | tf_op jit(solution)/shard_map/ppermute | solution.py:24
  16.6 16.1 %collective-permute-start.3 = (f32[53,4,2,128]{3,0,2,1:T(8,128)}, f32[53,4,2,128]{3,0,2,1:T(8,128)S(1)}, u32[]{:S(2)}, u32[]{:S(2)}) collective-permute-start(f32[53,4,2,128]{3,0,2,1:T(8,128)} %get-tuple-element.16), channel_id=1, source_target_pairs={{4,0},{8,4},{12,8},{0,12},{5,1},{9,5},{13,9},{1,13},{6,2},{10,6},{... | collective-permute-start | bytes 651272 | tf_op jit(solution)/shard_map/ppermute | solution.py:25
  116.5 9.9 %collective-permute-start.10 = (f32[53,4,4,2]{3,0,2,1:T(8,128)S(1)}, f32[53,4,4,2]{3,0,2,1:T(8,128)}, u32[]{:S(2)}, u32[]{:S(2)}) collective-permute-start(f32[53,4,4,2]{3,0,2,1:T(8,128)S(1)} %get-tuple-element.6), channel_id=1, source_target_pairs={{0,1},{1,2},{2,3},{3,0},{4,5},{5,6},{6,7},{7,4},{8,9},{9,10},{10,1... | collective-permute-start | bytes 20360 | tf_op jit(solution)/shard_map/ppermute | solution.py:24
  119.8 13.1 %collective-permute-start.11 = (f32[53,4,4,2]{3,0,2,1:T(8,128)S(1)}, f32[53,4,4,2]{3,0,2,1:T(8,128)}, u32[]{:S(2)}, u32[]{:S(2)}) collective-permute-start(f32[53,4,4,2]{3,0,2,1:T(8,128)S(1)} %get-tuple-element.5), channel_id=1, source_target_pairs={{1,0},{2,1},{3,2},{0,3},{5,4},{6,5},{7,6},{4,7},{9,8},{10,9},{11,1... | collective-permute-start | bytes 20360 | tf_op jit(solution)/shard_map/ppermute | solution.py:25
  120.5 13.6 %collective-permute-start.6 = (f32[53,2,4,128]{3,0,2,1:T(8,128)}, f32[53,2,4,128]{3,0,2,1:T(8,128)S(1)}, u32[]{:S(2)}, u32[]{:S(2)}) collective-permute-start(f32[53,2,4,128]{3,0,2,1:T(8,128)} %get-tuple-element.7), channel_id=1, source_target_pairs={{0,16},{16,32},{32,48},{48,64},{64,80},{80,96},{96,112},{112,0},{1... | collective-permute-start | bytes 651272 | tf_op jit(solution)/shard_map/ppermute | solution.py:24
  121.1 17.3 %collective-permute-start.7 = (f32[53,2,4,128]{3,0,2,1:T(8,128)}, f32[53,2,4,128]{3,0,2,1:T(8,128)S(1)}, u32[]{:S(2)}, u32[]{:S(2)}) collective-permute-start(f32[53,2,4,128]{3,0,2,1:T(8,128)} %get-tuple-element.8), channel_id=1, source_target_pairs={{16,0},{32,16},{48,32},{64,48},{80,64},{96,80},{112,96},{0,112},{1... | collective-permute-start | bytes 651272 | tf_op jit(solution)/shard_map/ppermute | solution.py:25
  125.7 13.8 %collective-permute-start.8 = (f32[53,4,2,128]{3,0,2,1:T(8,128)S(1)}, f32[53,4,2,128]{3,0,2,1:T(8,128)S(1)}, u32[]{:S(2)}, u32[]{:S(2)}) collective-permute-start(f32[53,4,2,128]{3,0,2,1:T(8,128)S(1)} %get-tuple-element.9), channel_id=1, source_target_pairs={{0,4},{4,8},{8,12},{12,0},{1,5},{5,9},{9,13},{13,1},{2,6},{6,10},{... | collective-permute-start | bytes 651272 | tf_op jit(solution)/shard_map/ppermute | solution.py:24
  126.4 14.0 %collective-permute-start.9 = (f32[53,4,2,128]{3,0,2,1:T(8,128)}, f32[53,4,2,128]{3,0,2,1:T(8,128)S(1)}, u32[]{:S(2)}, u32[]{:S(2)}) collective-permute-start(f32[53,4,2,128]{3,0,2,1:T(8,128)} %get-tuple-element.10), channel_id=1, source_target_pairs={{4,0},{8,4},{12,8},{0,12},{5,1},{9,5},{13,9},{1,13},{6,2},{10,6},{... | collective-permute-start | bytes 651272 | tf_op jit(solution)/shard_map/ppermute | solution.py:25
where the time goes:
time: 230 us; the launch traced here: 228 us
  blocking collectives  98.9 us (43%)
  other arithmetic  63.8 us (28%)
  starting transfers between devices  22.1 us (10%)
  waiting for transfers between devices  16.8 us (7%)
  local copies, waits for them, and re-layouts  15.1 us (7%)
  matrix products  5.9 us (3%)
  between operations  4.95 us (2%)
    all_to_all x12, blocking collectives, from_everyone(): return lax.all_to_all(copies, axis, split_axis=0, concat_axis=0, tiled=True)  98.9 us
    unnamed x4, other arithmetic  40.2 us
    ppermute x6, starting transfers between devices, with_halo(): lax.ppermute(leading, axis, [(b, a) for a, b in up])  16 us
    ppermute x6, waiting for transfers between devices, with_halo(): lax.ppermute(leading, axis, [(b, a) for a, b in up])  9.01 us
    ppermute x6, waiting for transfers between devices, with_halo(): lax.ppermute(last, axis, up)  7.77 us
    broadcast_in_dim x12, local copies, waits for them, and re-layouts, from_everyone(): copies = jnp.broadcast_to(array, (lax.axis_size(axis), *array.shape))  7.76 us
    reduce_sum x12, other arithmetic, of_everyone(): return jnp.sum(everything, axis=0)  7.27 us
    select_n x6, other arithmetic, mirror_walls(): low_part = jnp.where(walled & (position == 0), low_edge, low_ghost)  6.13 us
  transfers between devices with their start and end apart: 12, of which 6 were waited for; matrix products, arithmetic and copies ran while one was open for 6% of the time, Pallas kernels for 0%

commit v1 on v0

v1 whole, which is shorter than its diff:
```python
import functools
import itertools

import jax
import jax.numpy as jnp
from jax import lax
from jax.experimental import pallas as pl
from jax.experimental.pallas import tpu as pltpu
from jax.sharding import PartitionSpec as P

MESH = pl.DeviceIdType.MESH
AXES = ("gx", "gy", "gz")

GAMMA = 0.2928932188134524
DELTA = -0.7071067811865475
REL_TOL = 0.1
ABS_TOL = 0.05
DRIFT = 0.2

S = 53
SP = 64
R = 16
L = 128
GROUP = 8
CHUNKS = 8


def offsets(sizes):
    out = []
    for off in itertools.product(*[range(n) for n in sizes]):
        if any(off):
            out.append(off)

    def hops(off):
        gx, gy, gz = off
        ring = lambda d, n: min(d % n, n - d % n)
        far_y = ring(gy, sizes[1])
        far_z = ring(gx // 2, sizes[0] // 2)
        far_x = ring(2 * (gx % 2) + gz // 2, 4)
        return far_x + far_y + far_z

    return sorted(out, key=lambda off: -hops(off))


def species_loop(fn, block=4):
    whole = S // block

    def body(i, carry):
        for k in range(block):
            fn(i * block + k)
        return carry

    lax.fori_loop(0, whole, body, 0)
    for s in range(whole * block, S):
        fn(s)


def kernel(
    sizes,
    state_hbm, diff_ref, rates_ref, inv_hbm, bound_ref,
    out_ref,
    st, inv, xlo, xhi, ya, yb, yra, yrb, zp, zlo, zhi,
    e0, ebuf, wts, base, zed, dee, gee, tbuf, cbuf, rpad, rows,
    load_sem, inv_sem, halo_send, halo_recv, norm_send, norm_recv,
):
    n_all = sizes[0] * sizes[1] * sizes[2]
    entries = float(S * R * L * n_all)
    pos = [lax.axis_index(a) for a in AXES]
    me = (pos[0] * sizes[1] + pos[1]) * sizes[2] + pos[2]

    def at(off):
        return {a: lax.rem(p + o, n) for a, p, o, n in zip(AXES, pos, off, sizes)}

    peers = offsets(sizes)

    load = pltpu.make_async_copy(state_hbm, st, load_sem)
    load.start()
    per = -(-S // CHUNKS)
    inv_loads = []
    for c in range(CHUNKS):
        lo, hi = c * per, min(S, (c + 1) * per)
        cp = pltpu.make_async_copy(inv_hbm.at[pl.ds(lo, hi - lo)], inv.at[pl.ds(lo, hi - lo)], inv_sem.at[c])
        cp.start()
        inv_loads.append(cp)

    barrier = pltpu.get_barrier_semaphore()
    for off in peers:
        pl.semaphore_signal(barrier, inc=1, device_id=at(off), device_id_type=MESH)

    row = lax.broadcasted_iota(jnp.int32, (8, L), 0)
    lane = lax.broadcasted_iota(jnp.int32, (8, L), 1)
    yy = lax.rem(row, 4)
    pp = lax.rem(lane, 4)
    f = lambda c: jnp.where(c, 1.0, 0.0).astype(jnp.float32)
    low_rows = f(row < 4)
    high_rows = f(row >= 4)

    def wall(d, edge):
        return jnp.where((bound_ref[d] == 0) & (pos[d] == edge), 1.0, 0.0).astype(jnp.float32)

    wx0, wx1 = wall(0, 0), wall(0, sizes[0] - 1)
    wy0, wy1 = wall(1, 0), wall(1, sizes[1] - 1)
    wz0, wz1 = wall(2, 0), wall(2, sizes[2] - 1)
    mx0, mx1, my0, my1, mz0, mz1 = [1.0 - w for w in (wx0, wx1, wy0, wy1, wz0, wz1)]

    rd = lambda ref, s, h: ref[s, pl.ds(8 * h, 8), :]

    def pack(field):
        def one(s):
            v0, v1 = rd(field, s, 0), rd(field, s, 1)
            ya[s] = jnp.where(yy < 2, pltpu.roll(v0, 6, 0), v1)
            yb[s] = jnp.where(yy < 2, v0, pltpu.roll(v1, 2, 0))

        species_loop(one)
        grp = lane // 4
        for q in range(4):
            h, s0 = q % 2, 32 * (q // 2)

            def body(k, acc):
                v = rd(field, s0 + k, h)
                return jnp.where(grp == k, pltpu.roll(v, 4 * k + 2, 1), acc)

            zp[pl.ds(8 * q, 8), :] = lax.fori_loop(0, min(32, S - s0), body, jnp.zeros((8, L), jnp.float32))

    def halo_copies(field, k):
        nx, ny, nz = sizes
        todo = [
            (field.at[:, pl.ds(8, 8), :], xlo.at[k], (1, 0, 0)),
            (field.at[:, pl.ds(0, 8), :], xhi.at[k], (nx - 1, 0, 0)),
            (ya, yra.at[k], (0, 1, 0)),
            (yb, yrb.at[k], (0, ny - 1, 0)),
            (zp, zlo.at[k], (0, 0, 1)),
            (zp, zhi.at[k], (0, 0, nz - 1)),
        ]
        cps = []
        for i, (src, dst, off) in enumerate(todo):
            cps.append(pltpu.make_async_remote_copy(
                src_ref=src, dst_ref=dst, send_sem=halo_send.at[k, i], recv_sem=halo_recv.at[k, i],
                device_id=at(off), device_id_type=MESH))
        return cps

    def inner(field, out):
        x0c = -30.0 + 16.0 * wx0 * low_rows
        x1c = -30.0 + 16.0 * wx1 * high_rows
        b1 = 16.0 * f(yy >= 1) - wy0 * f(yy == 1) - wy1 * f(yy == 3)
        bm1 = 16.0 * f(yy <= 2) - wy0 * f(yy == 0) - wy1 * f(yy == 2)
        b2, bm2 = -f(yy >= 2), -f(yy <= 1)
        a1 = 16.0 * f(lane >= 1) - wz0 * f(lane == 1) - wz1 * f(lane == L - 1)
        am1 = 16.0 * f(lane <= L - 2) - wz0 * f(lane == 0) - wz1 * f(lane == L - 2)
        a2, am2 = -f(lane >= 2), -f(lane <= L - 3)
        yz0 = (-60.0 + 16.0 * wy0 * f(yy == 0) + 16.0 * wy1 * f(yy == 3)
               + 16.0 * wz0 * f(lane == 0) + 16.0 * wz1 * f(lane == L - 1))
        own_drift = -DRIFT + DRIFT * wx0 * low_rows

        def one(s):
            c = diff_ref[s] * (1.0 / 12.0)
            v0, v1 = rd(field, s, 0), rd(field, s, 1)
            s0, s1 = pltpu.roll(v0, 4, 0), pltpu.roll(v1, 4, 0)

            def yz(v):
                return (yz0 * v + b1 * pltpu.roll(v, 1, 0) + b2 * pltpu.roll(v, 2, 0)
                        + bm1 * pltpu.roll(v, 7, 0) + bm2 * pltpu.roll(v, 6, 0)
                        + a1 * pltpu.roll(v, 1, 1) + a2 * pltpu.roll(v, 2, 1)
                        + am1 * pltpu.roll(v, L - 1, 1) + am2 * pltpu.roll(v, L - 2, 1))

            l0 = x0c * v0 + (16.0 - wx0) * s0 + 16.0 * high_rows * s1 - v1 + yz(v0)
            l1 = x1c * v1 + (16.0 - wx1) * s1 + 16.0 * low_rows * s0 - v0 + yz(v1)
            out[s, pl.ds(0, 8), :] = c * l0 + own_drift * v0 + DRIFT * high_rows * s0
            out[s, pl.ds(8, 8), :] = c * l1 - DRIFT * v1 + DRIFT * jnp.where(row >= 4, s1, s0)

        species_loop(one, 2)

    def outer(k, part, fin):
        edge = (lane < 2) | (lane >= L - 2)
        for q in range(4):
            lo = zlo[k, pl.ds(8 * q, 8), :]
            hi = zhi[k, pl.ds(8 * q, 8), :]
            from_hi = mz1 * (16.0 * f(pp == 1) * pltpu.roll(hi, L - 1, 1) - pltpu.roll(hi, L - 2, 1))
            from_lo = mz0 * (16.0 * f(pp == 2) * pltpu.roll(lo, 1, 1) - pltpu.roll(lo, 2, 1))
            zp[pl.ds(8 * q, 8), :] = jnp.where(pp < 2, from_hi, from_lo)
        even = 16.0 * my0 * f(lax.rem(row, 2) == 0)
        odd = 16.0 * my1 * f(lax.rem(row, 2) == 1)
        lo16, hi16, dr = 16.0 * mx0 * low_rows, 16.0 * mx1 * high_rows, DRIFT * mx0 * low_rows

        def one(s):
            c = diff_ref[s] * (1.0 / 12.0)
            xl, xh = xlo[k, s], xhi[k, s]
            a, b = yra[k, s], yrb[k, s]
            rl, rh = pltpu.roll(xl, 4, 0), pltpu.roll(xh, 4, 0)
            ca = even * pltpu.roll(a, 7, 0) - my0 * a
            cb = odd * pltpu.roll(b, 1, 0) - my1 * b
            q = 2 * (s // 32)
            g = lax.rem(s, 32)
            shift = lax.rem(2 * L - 2 - 4 * g, L)
            off = q * 8 if isinstance(q, int) else pl.multiple_of(q * 8, 8)
            z0 = pltpu.roll(zp[pl.ds(off, 8), :], shift, 1)
            z1 = pltpu.roll(zp[pl.ds(off + 8, 8), :], shift, 1)
            l0 = lo16 * rl - mx0 * xl + jnp.where(yy < 2, ca, pltpu.roll(cb, 2, 0)) + jnp.where(edge, z0, 0.0)
            l1 = hi16 * rh - mx1 * xh + jnp.where(yy < 2, pltpu.roll(ca, 6, 0), cb) + jnp.where(edge, z1, 0.0)
            fin(s, 0, rd(part, s, 0) + c * l0 + dr * rl)
            fin(s, 1, rd(part, s, 1) + c * l1)

        species_loop(one, 2)

    def put_tanh(s, h, v):
        start = s * R + 8 * h
        if not isinstance(s, int):
            start = pl.multiple_of(start, 8)
        tbuf[pl.ds(start, 8), :] = jnp.tanh(v)

    def chem_at(s, h):
        start = s * R + 8 * h
        if not isinstance(s, int):
            start = pl.multiple_of(start, 8)
        return cbuf[pl.ds(start, 8), :]

    def chemistry():
        lhs = rows_lhs()
        for r in range(0, R, 2):
            t = jnp.concatenate([tbuf[pl.ds(r + i, SP, stride=R), :] for i in range(2)], axis=1)
            hi = t.astype(jnp.bfloat16)
            lo = (t - hi.astype(jnp.float32)).astype(jnp.bfloat16)
            got = jnp.dot(lhs, jnp.concatenate([hi, lo, hi, lo], axis=0), preferred_element_type=jnp.float32)
            for i in range(2):
                cbuf[pl.ds(r + i, SP, stride=R), :] = got[:, i * L:(i + 1) * L]

    def rows_lhs():
        both = rpad[...] + pltpu.roll(rpad[...], SP, 1)
        hi = both.astype(jnp.bfloat16)
        lo = (both - hi.astype(jnp.float32)).astype(jnp.bfloat16)
        return jnp.concatenate([hi, lo], axis=1)

    def matvec():
        last = S - GROUP
        steps = -(-S // GROUP)

        def body(i, carry):
            h = lax.rem(i, 2)
            s0 = jnp.minimum((i // 2) * GROUP, last)
            at_rows = pl.ds(pl.multiple_of(h * 8, 8), 8)
            acc = None
            for j in range(S):
                term = inv[pl.ds(s0, GROUP), j, at_rows, :] * gee[j, at_rows, :][None]
                acc = term if acc is None else acc + term
            dee[pl.ds(s0, GROUP), at_rows, :] = acc
            return carry

        lax.fori_loop(0, 2 * steps, body, 0)

    def damping(k):
        def body(s, acc):
            u = dee[s] * wts[s]
            u = u * u
            return acc + u[0:8] + u[8:16]

        acc = lax.fori_loop(0, S, body, jnp.zeros((8, L), jnp.float32))
        rows[k, pl.ds(me, 1), :] = jnp.sum(acc, axis=0, keepdims=True)
        for off in peers:
            pltpu.make_async_remote_copy(
                src_ref=rows.at[k, pl.ds(me, 1), :], dst_ref=rows.at[k, pl.ds(me, 1), :],
                send_sem=norm_send.at[k], recv_sem=norm_recv.at[k],
                device_id=at(off), device_id_type=MESH).start()
        count = len(peers)
        all_rows = pltpu.make_async_remote_copy(
            src_ref=rows.at[k, pl.ds(0, count), :], dst_ref=rows.at[k, pl.ds(0, count), :],
            send_sem=norm_send.at[k], recv_sem=norm_recv.at[k],
            device_id=at(peers[0]), device_id_type=MESH)
        all_rows.wait_recv()
        all_rows.wait_send()
        total = jnp.sum(jnp.sum(rows[k], axis=0, keepdims=True), axis=1, keepdims=True)
        return 1.0 / jnp.maximum(jnp.sqrt(total * (1.0 / entries)), 1.0)

    halves = [(0, pl.ds(0, 8)), (1, pl.ds(8, 8))]

    def newton(k, last):
        chemistry()

        def first(s):
            for h, hs in halves:
                gee[s, hs, :] = -GAMMA * chem_at(s, h)

        species_loop(first)
        if k == 0:
            for cp in inv_loads:
                cp.wait()
        matvec()
        r = damping(k)

        def mid(s):
            for h, hs in halves:
                z = base[s, hs, :] - dee[s, hs, :] * r
                zed[s, hs, :] = z
                put_tanh(s, h, z)

        species_loop(mid)
        chemistry()

        def second(s):
            for h, hs in halves:
                gee[s, hs, :] = zed[s, hs, :] - base[s, hs, :] - GAMMA * chem_at(s, h)

        species_loop(second)
        matvec()
        r2 = damping(k + 1)

        def end(s):
            for h, hs in halves:
                last(s, h, zed[s, hs, :] - dee[s, hs, :] * r2)

        species_loop(end)

    tbuf[pl.ds(S * R, (SP - S) * R), :] = jnp.zeros(((SP - S) * R, L), jnp.float32)
    rpad[...] = jnp.zeros((SP, L), jnp.float32)
    rpad[0:S, 0:S] = rates_ref[...]
    load.wait()
    pack(st)
    pl.semaphore_wait(barrier, len(peers))
    cps = halo_copies(st, 0)
    for cp in cps:
        cp.start()
    inner(st, e0)

    def weigh(s):
        wts[s] = 1.0 / (REL_TOL * jnp.abs(st[s]) + ABS_TOL)

    species_loop(weigh)
    for cp in cps:
        cp.wait()

    def fin0(s, h, e):
        hs = pl.ds(8 * h, 8)
        e0[s, hs, :] = e
        b = st[s, hs, :] + GAMMA * e
        base[s, hs, :] = b
        put_tanh(s, h, b)

    outer(0, e0, fin0)

    def keep(s, h, v):
        gee[s, pl.ds(8 * h, 8), :] = v
        put_tanh(s, h, v)

    newton(0, keep)

    pack(gee)
    cps = halo_copies(gee, 1)
    for cp in cps:
        cp.start()
    inner(gee, ebuf)
    chemistry()

    def pre(s):
        for h, hs in halves:
            base[s, hs, :] = st[s, hs, :] + DELTA * e0[s, hs, :] + (1.0 - GAMMA) * chem_at(s, h)

    species_loop(pre)
    for cp in cps:
        cp.wait()

    def fin1(s, h, e):
        hs = pl.ds(8 * h, 8)
        b = base[s, hs, :] + (1.0 - DELTA) * e
        base[s, hs, :] = b
        put_tanh(s, h, b)

    outer(1, ebuf, fin1)

    def give(s, h, v):
        out_ref[s, pl.ds(8 * h, 8), :] = v

    newton(2, give)


def body(sizes, state, diffusivity, rates, inverse, boundary):
    shape = state.shape
    field = pltpu.VMEM((S, R, L), jnp.float32)
    face = pltpu.VMEM((S, 8, L), jnp.float32)
    faces = pltpu.VMEM((2, S, 8, L), jnp.float32)
    n_all = sizes[0] * sizes[1] * sizes[2]
    out = pl.pallas_call(
        functools.partial(kernel, sizes),
        name="ark_step",
        out_shape=jax.ShapeDtypeStruct((S, R, L), jnp.float32),
        in_specs=[
            pl.BlockSpec(memory_space=pl.ANY),
            pl.BlockSpec(memory_space=pltpu.SMEM),
            pl.BlockSpec(memory_space=pltpu.VMEM),
            pl.BlockSpec(memory_space=pl.ANY),
            pl.BlockSpec(memory_space=pltpu.SMEM),
        ],
        out_specs=pl.BlockSpec(memory_space=pltpu.VMEM),
        scratch_shapes=[
            field, pltpu.VMEM((S, S, R, L), jnp.float32),
            faces, faces, face, face, faces, faces,
            pltpu.VMEM((32, L), jnp.float32), pltpu.VMEM((2, 32, L), jnp.float32), pltpu.VMEM((2, 32, L), jnp.float32),
            field, field, field, field, field, field, field,
            pltpu.VMEM((SP * R, L), jnp.float32), pltpu.VMEM((SP * R, L), jnp.float32),
            pltpu.VMEM((SP, L), jnp.float32), pltpu.VMEM((4, n_all, L), jnp.float32),
            pltpu.SemaphoreType.DMA, pltpu.SemaphoreType.DMA((CHUNKS,)),
            pltpu.SemaphoreType.DMA((2, 6)), pltpu.SemaphoreType.DMA((2, 6)),
            pltpu.SemaphoreType.DMA((4,)), pltpu.SemaphoreType.DMA((4,)),
        ],
        compiler_params=pltpu.CompilerParams(collective_id=0, has_side_effects=True),
    )(
        state.reshape(S, R, L), diffusivity, rates, inverse.reshape(S, S, R, L), boundary,
    )
    return out.reshape(shape)


def solution(mesh):
    sizes = tuple(mesh.shape[a] for a in AXES)
    in_specs = (P(None, "gx", "gy", "gz"), P(), P(), P(None, None, "gx", "gy", "gz"), P())
    return jax.shard_map(
        functools.partial(body, sizes), mesh=mesh, in_specs=in_specs, out_specs=P(None, "gx", "gy", "gz"), check_vma=False)
```

time: 230 us -> 100 us (0.43); the launches traced: 228 us -> 99.9 us
  blocking collectives: 98.9 us -> 0 us
  Pallas kernels: 0 us -> 98.1 us
  other arithmetic: 63.8 us -> 0 us
  starting transfers between devices: 22.1 us -> 0 us
  waiting for transfers between devices: 16.8 us -> 0 us
  local copies, waits for them, and re-layouts: 15.1 us -> 1.8 us
  matrix products: 5.9 us -> 0 us
  between operations: 4.95 us -> 0.01 us
    all_to_all x12 -> x0, blocking collectives: 98.9 us -> none  [from_everyone(): return lax.all_to_all(copies, axis, split_axis=0, concat_axis=0, tiled=True)]
    pallas_call x0 -> x1, Pallas kernels: none -> 98.1 us  [body(): pl.pallas_call(functools.partial(kernel, sizes), name='ark_step', out_sha...]
    unnamed x4 -> x0, other arithmetic: 40.2 us -> none
    ppermute x12 -> x0, starting transfers between devices: 22.1 us -> none  [the longest x6 16 us: with_halo(): lax.ppermute(leading, axis, [(b, a) for a, b in up])]
    ppermute x12 -> x0, waiting for transfers between devices: 16.8 us -> none  [the longest x6 9.01 us: with_halo(): lax.ppermute(leading, axis, [(b, a) for a, b in up])]
    reduce_sum x16 -> x0, other arithmetic: 11 us -> none  [the longest x12 7.27 us: of_everyone(): return jnp.sum(everything, axis=0)]
    select_n x12 -> x0, other arithmetic: 10.4 us -> none  [the longest x6 6.13 us: mirror_walls(): low_part = jnp.where(walled & (position == 0), low_edge, low_ghost)]
    broadcast_in_dim x12 -> x0, local copies, waits for them, and re-layouts: 7.76 us -> none  [from_everyone(): copies = jnp.broadcast_to(array, (lax.axis_size(axis), *array.shape))]
  transfers between devices with their start and end apart: 12 -> 0, of which waited for: 6 -> 0; matrix products, arithmetic and copies ran while one was open for 6% -> 0% of each run, Pallas kernels for 0% -> 0%
where the time goes in v1:
time: 100 us; the launch traced here: 99.9 us
  Pallas kernels  98.1 us (98%)
  local copies, waits for them, and re-layouts  1.8 us (2%)
    pallas_call x1, Pallas kernels, body(): pl.pallas_call(functools.partial(kernel, sizes), name='ark_step', out_sha...  98.1 us

profile of v1, /device:TPU:1, one launch (start us, length us, event | category | flops | bytes accessed | tf_op | source)
XLA Modules:
  0.0 99.9 jit_solution(17543637865418368557)
XLA Ops:
  0.0 98.1 %ark_step.1 = f32[53,16,128]{2,1,0:T(8,128)} custom-call(f32[53,16,128]{2,1,0:T(8,128)} %bitcast.5, f32[53]{0:T(128)} %diff_ref.1, f32[53,53]{1,0:T(8,128)} %rates_ref.1, f32[53,53,16,128]{3,2,1,0:T(8,128)} %bitcast.3, s32[3]{0:T(128)} %bound_ref.1), custom_call_target="tpu_custom_call" | custom-call | tf_op jit(solution)/shard_map/ark_step/pallas_call | solution.py:380
  98.1 1.8 %copy.7 = f32[53,4,4,128]{3,2,1,0:T(4,128)} copy(f32[53,4,4,128]{3,2,1,0:T(4,128)} %bitcast.4) | data formatting | bytes 868352

commit v2 on v1

--- a/solution.py
+++ b/solution.py
@@ -21,7 +21,8 @@
 SP = 64
 R = 16
 L = 128
-GROUP = 8
+GROUP = 9
+JB = 8
 CHUNKS = 8
 
 
@@ -55,13 +56,28 @@
         fn(s)
 
 
+def block_loop(fn, block=16):
+    whole = S // block
+
+    def body(i, carry):
+        fn(i, [i * block + k for k in range(block)])
+        return carry
+
+    lax.fori_loop(0, whole, body, 0)
+    fn(whole, list(range(whole * block, S)))
+
+
+def tile8(i):
+    return pl.ds(8 * i if isinstance(i, int) else pl.multiple_of(8 * i, 8), 8)
+
+
 def kernel(
     sizes,
     state_hbm, diff_ref, rates_ref, inv_hbm, bound_ref,
     out_ref,
-    st, inv, xlo, xhi, ya, yb, yra, yrb, zp, zlo, zhi,
-    e0, ebuf, wts, base, zed, dee, gee, tbuf, cbuf, rpad, rows,
-    load_sem, inv_sem, halo_send, halo_recv, norm_send, norm_recv,
+    st, inv, xlo, xhi, ya, yb, yra, yrb, zp, zk, zlo, zhi,
+    e0, ebuf, wts, base, zed, sec, dee, gee, tbuf, cbuf, rpad, rows,
+    load_sem, inv_sem, halo_send, halo_recv, norm_send, norm_recv, ready,
 ):
     n_all = sizes[0] * sizes[1] * sizes[2]
     entries = float(S * R * L * n_all)
@@ -84,8 +100,14 @@
         inv_loads.append(cp)
 
     barrier = pltpu.get_barrier_semaphore()
-    for off in peers:
+    lines = [[tuple(o if a == d else 0 for a in range(3)) for o in range(1, sizes[d])] for d in range(3)]
+    near = lines[0] + lines[1] + lines[2]
+    for off in near:
         pl.semaphore_signal(barrier, inc=1, device_id=at(off), device_id_type=MESH)
+
+    def tell(i, line):
+        for off in line:
+            pl.semaphore_signal(ready.at[i], inc=1, device_id=at(off), device_id_type=MESH)
 
     row = lax.broadcasted_iota(jnp.int32, (8, L), 0)
     lane = lax.broadcasted_iota(jnp.int32, (8, L), 1)
@@ -105,32 +127,30 @@
 
     rd = lambda ref, s, h: ref[s, pl.ds(8 * h, 8), :]
 
-    def pack(field):
-        def one(s):
-            v0, v1 = rd(field, s, 0), rd(field, s, 1)
-            ya[s] = jnp.where(yy < 2, pltpu.roll(v0, 6, 0), v1)
-            yb[s] = jnp.where(yy < 2, v0, pltpu.roll(v1, 2, 0))
-
-        species_loop(one)
-        grp = lane // 4
-        for q in range(4):
-            h, s0 = q % 2, 32 * (q // 2)
-
-            def body(k, acc):
-                v = rd(field, s0 + k, h)
-                return jnp.where(grp == k, pltpu.roll(v, 4 * k + 2, 1), acc)
-
-            zp[pl.ds(8 * q, 8), :] = lax.fori_loop(0, min(32, S - s0), body, jnp.zeros((8, L), jnp.float32))
+    grp = lane // 4
+
+    def pack(field, k):
+        def some(i, species):
+            acc = jnp.zeros((8, L), jnp.float32)
+            for g, s in enumerate(species):
+                v0, v1 = rd(field, s, 0), rd(field, s, 1)
+                ya[k, s] = jnp.where(yy < 2, pltpu.roll(v0, 6, 0), v1)
+                yb[k, s] = jnp.where(yy < 2, v0, pltpu.roll(v1, 2, 0))
+                acc = jnp.where(grp == 2 * g, pltpu.roll(v0, (8 * g + 2) % L, 1), acc)
+                acc = jnp.where(grp == 2 * g + 1, pltpu.roll(v1, (8 * g + 6) % L, 1), acc)
+            zp[k, tile8(i), :] = acc
+
+        block_loop(some)
 
     def halo_copies(field, k):
         nx, ny, nz = sizes
         todo = [
             (field.at[:, pl.ds(8, 8), :], xlo.at[k], (1, 0, 0)),
             (field.at[:, pl.ds(0, 8), :], xhi.at[k], (nx - 1, 0, 0)),
-            (ya, yra.at[k], (0, 1, 0)),
-            (yb, yrb.at[k], (0, ny - 1, 0)),
-            (zp, zlo.at[k], (0, 0, 1)),
-            (zp, zhi.at[k], (0, 0, nz - 1)),
+            (zp.at[k], zlo.at[k], (0, 0, 1)),
+            (zp.at[k], zhi.at[k], (0, 0, nz - 1)),
+            (ya.at[k], yra.at[k], (0, 1, 0)),
+            (yb.at[k], yrb.at[k], (0, ny - 1, 0)),
         ]
         cps = []
         for i, (src, dst, off) in enumerate(todo):
@@ -168,7 +188,7 @@
             out[s, pl.ds(0, 8), :] = c * l0 + own_drift * v0 + DRIFT * high_rows * s0
             out[s, pl.ds(8, 8), :] = c * l1 - DRIFT * v1 + DRIFT * jnp.where(row >= 4, s1, s0)
 
-        species_loop(one, 2)
+        species_loop(one, 4)
 
     def outer(k, part, fin):
         edge = (lane < 2) | (lane >= L - 2)
@@ -177,30 +197,28 @@
             hi = zhi[k, pl.ds(8 * q, 8), :]
             from_hi = mz1 * (16.0 * f(pp == 1) * pltpu.roll(hi, L - 1, 1) - pltpu.roll(hi, L - 2, 1))
             from_lo = mz0 * (16.0 * f(pp == 2) * pltpu.roll(lo, 1, 1) - pltpu.roll(lo, 2, 1))
-            zp[pl.ds(8 * q, 8), :] = jnp.where(pp < 2, from_hi, from_lo)
+            zk[pl.ds(8 * q, 8), :] = jnp.where(pp < 2, from_hi, from_lo)
         even = 16.0 * my0 * f(lax.rem(row, 2) == 0)
         odd = 16.0 * my1 * f(lax.rem(row, 2) == 1)
         lo16, hi16, dr = 16.0 * mx0 * low_rows, 16.0 * mx1 * high_rows, DRIFT * mx0 * low_rows
 
-        def one(s):
-            c = diff_ref[s] * (1.0 / 12.0)
-            xl, xh = xlo[k, s], xhi[k, s]
-            a, b = yra[k, s], yrb[k, s]
-            rl, rh = pltpu.roll(xl, 4, 0), pltpu.roll(xh, 4, 0)
-            ca = even * pltpu.roll(a, 7, 0) - my0 * a
-            cb = odd * pltpu.roll(b, 1, 0) - my1 * b
-            q = 2 * (s // 32)
-            g = lax.rem(s, 32)
-            shift = lax.rem(2 * L - 2 - 4 * g, L)
-            off = q * 8 if isinstance(q, int) else pl.multiple_of(q * 8, 8)
-            z0 = pltpu.roll(zp[pl.ds(off, 8), :], shift, 1)
-            z1 = pltpu.roll(zp[pl.ds(off + 8, 8), :], shift, 1)
-            l0 = lo16 * rl - mx0 * xl + jnp.where(yy < 2, ca, pltpu.roll(cb, 2, 0)) + jnp.where(edge, z0, 0.0)
-            l1 = hi16 * rh - mx1 * xh + jnp.where(yy < 2, pltpu.roll(ca, 6, 0), cb) + jnp.where(edge, z1, 0.0)
-            fin(s, 0, rd(part, s, 0) + c * l0 + dr * rl)
-            fin(s, 1, rd(part, s, 1) + c * l1)
-
-        species_loop(one, 2)
+        def some(i, species):
+            zt = zk[tile8(i), :]
+            for g, s in enumerate(species):
+                c = diff_ref[s] * (1.0 / 12.0)
+                xl, xh = xlo[k, s], xhi[k, s]
+                a, b = yra[k, s], yrb[k, s]
+                rl, rh = pltpu.roll(xl, 4, 0), pltpu.roll(xh, 4, 0)
+                ca = even * pltpu.roll(a, 7, 0) - my0 * a
+                cb = odd * pltpu.roll(b, 1, 0) - my1 * b
+                z0 = pltpu.roll(zt, (2 * L - 2 - 8 * g) % L, 1)
+                z1 = pltpu.roll(zt, (2 * L - 6 - 8 * g) % L, 1)
+                l0 = lo16 * rl - mx0 * xl + jnp.where(yy < 2, ca, pltpu.roll(cb, 2, 0)) + jnp.where(edge, z0, 0.0)
+                l1 = hi16 * rh - mx1 * xh + jnp.where(yy < 2, pltpu.roll(ca, 6, 0), cb) + jnp.where(edge, z1, 0.0)
+                fin(s, 0, rd(part, s, 0) + c * l0 + dr * rl)
+                fin(s, 1, rd(part, s, 1) + c * l1)
+
+        block_loop(some)
 
     def put_tanh(s, h, v):
         start = s * R + 8 * h
@@ -233,42 +251,48 @@
     def matvec():
         last = S - GROUP
         steps = -(-S // GROUP)
-
-        def body(i, carry):
-            h = lax.rem(i, 2)
-            s0 = jnp.minimum((i // 2) * GROUP, last)
-            at_rows = pl.ds(pl.multiple_of(h * 8, 8), 8)
-            acc = None
-            for j in range(S):
-                term = inv[pl.ds(s0, GROUP), j, at_rows, :] * gee[j, at_rows, :][None]
-                acc = term if acc is None else acc + term
-            dee[pl.ds(s0, GROUP), at_rows, :] = acc
-            return carry
-
-        lax.fori_loop(0, 2 * steps, body, 0)
-
-    def damping(k):
-        def body(s, acc):
-            u = dee[s] * wts[s]
-            u = u * u
-            return acc + u[0:8] + u[8:16]
-
-        acc = lax.fori_loop(0, S, body, jnp.zeros((8, L), jnp.float32))
-        rows[k, pl.ds(me, 1), :] = jnp.sum(acc, axis=0, keepdims=True)
+        again = steps * GROUP - S
+
+        def columns(s0, j0, count, accs):
+            accs = list(accs)
+            for jj in range(count):
+                g = gee[j0 + jj]
+                for k in range(GROUP):
+                    accs[k] = accs[k] + inv[s0 + k, j0 + jj] * g
+            return tuple(accs)
+
+        def body(i, total):
+            s0 = jnp.minimum(i * GROUP, last)
+            accs = tuple(jnp.zeros((R, L), jnp.float32) for _ in range(GROUP))
+            accs = lax.fori_loop(0, S // JB, lambda t, acc: columns(s0, t * JB, JB, acc), accs)
+            accs = columns(s0, S // JB * JB, S % JB, accs)
+            fresh = jnp.where(i == steps - 1, 0.0, 1.0)
+            for k in range(GROUP):
+                dee[s0 + k] = accs[k]
+                u = accs[k] * wts[s0 + k]
+                u = u * u
+                total = total + (u * fresh if k < again else u)
+            return total
+
+        return lax.fori_loop(0, steps, body, jnp.zeros((R, L), jnp.float32))
+
+    def damping(k, total):
+        rows[k, pl.ds(me, 1), :] = jnp.sum(total, axis=0, keepdims=True)
         for off in peers:
             pltpu.make_async_remote_copy(
                 src_ref=rows.at[k, pl.ds(me, 1), :], dst_ref=rows.at[k, pl.ds(me, 1), :],
                 send_sem=norm_send.at[k], recv_sem=norm_recv.at[k],
                 device_id=at(off), device_id_type=MESH).start()
+        all_rows(k).wait_recv()
+        total = jnp.sum(jnp.sum(rows[k], axis=0, keepdims=True), axis=1, keepdims=True)
+        return 1.0 / jnp.maximum(jnp.sqrt(total * (1.0 / entries)), 1.0)
+
+    def all_rows(k):
         count = len(peers)
-        all_rows = pltpu.make_async_remote_copy(
+        return pltpu.make_async_remote_copy(
             src_ref=rows.at[k, pl.ds(0, count), :], dst_ref=rows.at[k, pl.ds(0, count), :],
             send_sem=norm_send.at[k], recv_sem=norm_recv.at[k],
             device_id=at(peers[0]), device_id_type=MESH)
-        all_rows.wait_recv()
-        all_rows.wait_send()
-        total = jnp.sum(jnp.sum(rows[k], axis=0, keepdims=True), axis=1, keepdims=True)
-        return 1.0 / jnp.maximum(jnp.sqrt(total * (1.0 / entries)), 1.0)
 
     halves = [(0, pl.ds(0, 8)), (1, pl.ds(8, 8))]
 
@@ -283,8 +307,10 @@
         if k == 0:
             for cp in inv_loads:
                 cp.wait()
-        matvec()
-        r = damping(k)
+        total = matvec()
+        if k == 0:
+            pl.semaphore_wait(ready.at[1], len(lines[0]))
+        r = damping(k, total)
 
         def mid(s):
             for h, hs in halves:
@@ -300,8 +326,7 @@
                 gee[s, hs, :] = zed[s, hs, :] - base[s, hs, :] - GAMMA * chem_at(s, h)
 
         species_loop(second)
-        matvec()
-        r2 = damping(k + 1)
+        r2 = damping(k + 1, matvec())
 
         def end(s):
             for h, hs in halves:
@@ -313,19 +338,22 @@
     rpad[...] = jnp.zeros((SP, L), jnp.float32)
     rpad[0:S, 0:S] = rates_ref[...]
     load.wait()
-    pack(st)
-    pl.semaphore_wait(barrier, len(peers))
-    cps = halo_copies(st, 0)
-    for cp in cps:
+    pack(st, 0)
+    pl.semaphore_wait(barrier, len(near))
+    first_halo = halo_copies(st, 0)
+    for cp in first_halo:
         cp.start()
+    tell(0, lines[1])
     inner(st, e0)
+    pl.semaphore_wait(ready.at[0], len(lines[1]))
+    tell(1, lines[0])
 
     def weigh(s):
         wts[s] = 1.0 / (REL_TOL * jnp.abs(st[s]) + ABS_TOL)
 
     species_loop(weigh)
-    for cp in cps:
-        cp.wait()
+    for cp in first_halo:
+        cp.wait_recv()
 
     def fin0(s, h, e):
         hs = pl.ds(8 * h, 8)
@@ -337,16 +365,18 @@
     outer(0, e0, fin0)
 
     def keep(s, h, v):
-        gee[s, pl.ds(8 * h, 8), :] = v
+        sec[s, pl.ds(8 * h, 8), :] = v
         put_tanh(s, h, v)
 
     newton(0, keep)
 
-    pack(gee)
-    cps = halo_copies(gee, 1)
-    for cp in cps:
+    second_halo = halo_copies(sec, 1)
+    for cp in second_halo[:2]:
         cp.start()
-    inner(gee, ebuf)
+    pack(sec, 1)
+    for cp in second_halo[2:]:
+        cp.start()
+    inner(sec, ebuf)
     chemistry()
 
     def pre(s):
@@ -354,8 +384,8 @@
             base[s, hs, :] = st[s, hs, :] + DELTA * e0[s, hs, :] + (1.0 - GAMMA) * chem_at(s, h)
 
     species_loop(pre)
-    for cp in cps:
-        cp.wait()
+    for cp in second_halo:
+        cp.wait_recv()
 
     def fin1(s, h, e):
         hs = pl.ds(8 * h, 8)
@@ -369,12 +399,15 @@
         out_ref[s, pl.ds(8 * h, 8), :] = v
 
     newton(2, give)
+    for cp in first_halo + second_halo:
+        cp.wait_send()
+    for k in range(4):
+        all_rows(k).wait_send()
 
 
 def body(sizes, state, diffusivity, rates, inverse, boundary):
     shape = state.shape
     field = pltpu.VMEM((S, R, L), jnp.float32)
-    face = pltpu.VMEM((S, 8, L), jnp.float32)
     faces = pltpu.VMEM((2, S, 8, L), jnp.float32)
     n_all = sizes[0] * sizes[1] * sizes[2]
     out = pl.pallas_call(
@@ -391,14 +424,15 @@
         out_specs=pl.BlockSpec(memory_space=pltpu.VMEM),
         scratch_shapes=[
             field, pltpu.VMEM((S, S, R, L), jnp.float32),
-            faces, faces, face, face, faces, faces,
-            pltpu.VMEM((32, L), jnp.float32), pltpu.VMEM((2, 32, L), jnp.float32), pltpu.VMEM((2, 32, L), jnp.float32),
-            field, field, field, field, field, field, field,
+            faces, faces, faces, faces, faces, faces,
+            pltpu.VMEM((2, 32, L), jnp.float32), pltpu.VMEM((32, L), jnp.float32),
+            pltpu.VMEM((2, 32, L), jnp.float32), pltpu.VMEM((2, 32, L), jnp.float32),
+            field, field, field, field, field, field, field, field,
             pltpu.VMEM((SP * R, L), jnp.float32), pltpu.VMEM((SP * R, L), jnp.float32),
             pltpu.VMEM((SP, L), jnp.float32), pltpu.VMEM((4, n_all, L), jnp.float32),
             pltpu.SemaphoreType.DMA, pltpu.SemaphoreType.DMA((CHUNKS,)),
             pltpu.SemaphoreType.DMA((2, 6)), pltpu.SemaphoreType.DMA((2, 6)),
-            pltpu.SemaphoreType.DMA((4,)), pltpu.SemaphoreType.DMA((4,)),
+            pltpu.SemaphoreType.DMA((4,)), pltpu.SemaphoreType.DMA((4,)), pltpu.SemaphoreType.REGULAR((2,)),
         ],
         compiler_params=pltpu.CompilerParams(collective_id=0, has_side_effects=True),
     )(

time: 100 us -> 75.9 us (0.76)
  Pallas kernels: 98.1 us -> 73.9 us
    pallas_call x1, Pallas kernels: 98.1 us -> 73.9 us  [body(): pl.pallas_call(functools.partial(kernel, sizes), name='ark_step', out_sha...]
where the time goes in v2:
time: 75.9 us; the launch traced here: 75.7 us
  Pallas kernels  73.9 us (97%)
  local copies, waits for them, and re-layouts  1.8 us (2%)
    pallas_call x1, Pallas kernels, body(): pl.pallas_call(functools.partial(kernel, sizes), name='ark_step', out_sha...  73.9 us
    unnamed x1, local copies, waits for them, and re-layouts  1.8 us

profile of v2, /device:TPU:1, one launch (start us, length us, event | category | flops | bytes accessed | tf_op | source)
XLA Modules:
  0.0 75.7 jit_solution(9253158065285892629)
XLA Ops:
  0.0 73.9 %ark_step.1 = f32[53,16,128]{2,1,0:T(8,128)} custom-call(f32[53,16,128]{2,1,0:T(8,128)} %bitcast.5, f32[53]{0:T(128)} %diff_ref.1, f32[53,53]{1,0:T(8,128)} %rates_ref.1, f32[53,53,16,128]{3,2,1,0:T(8,128)} %bitcast.3, s32[3]{0:T(128)} %bound_ref.1), custom_call_target="tpu_custom_call" | custom-call | tf_op jit(solution)/shard_map/ark_step/pallas_call | solution.py:413
  73.9 1.8 %copy.7 = f32[53,4,4,128]{3,2,1,0:T(4,128)} copy(f32[53,4,4,128]{3,2,1,0:T(4,128)} %bitcast.4) | data formatting | bytes 868352

commit v3 on v2

--- a/solution.py
+++ b/solution.py
@@ -21,7 +21,7 @@
 SP = 64
 R = 16
 L = 128
-GROUP = 9
+GROUP = 18
 JB = 8
 CHUNKS = 8
 
@@ -73,9 +73,9 @@
 
 def kernel(
     sizes,
-    state_hbm, diff_ref, rates_ref, inv_hbm, bound_ref,
+    state_hbm, diff_hbm, rates_hbm, inv_hbm, bound_hbm,
     out_ref,
-    st, inv, xlo, xhi, ya, yb, yra, yrb, zp, zk, zlo, zhi,
+    diff_ref, rates_ref, bound_ref, st, inv, xlo, xhi, ya, yb, yra, yrb, zp, zk, zlo, zhi,
     e0, ebuf, wts, base, zed, sec, dee, gee, tbuf, cbuf, rpad, rows,
     load_sem, inv_sem, halo_send, halo_recv, norm_send, norm_recv, ready,
 ):
@@ -89,8 +89,18 @@
 
     peers = offsets(sizes)
 
-    load = pltpu.make_async_copy(state_hbm, st, load_sem)
+    barrier = pltpu.get_barrier_semaphore()
+    lines = [[tuple(o if a == d else 0 for a in range(3)) for o in range(1, sizes[d])] for d in range(3)]
+    near = lines[0] + lines[1] + lines[2]
+    for off in near:
+        pl.semaphore_signal(barrier, inc=1, device_id=at(off), device_id_type=MESH)
+
+    load = pltpu.make_async_copy(state_hbm, st, load_sem.at[0])
     load.start()
+    small = [pltpu.make_async_copy(src, dst, load_sem.at[i]) for i, (src, dst) in enumerate(
+        [(diff_hbm, diff_ref), (rates_hbm, rates_ref), (bound_hbm, bound_ref)], 1)]
+    for cp in small:
+        cp.start()
     per = -(-S // CHUNKS)
     inv_loads = []
     for c in range(CHUNKS):
@@ -99,15 +109,12 @@
         cp.start()
         inv_loads.append(cp)
 
-    barrier = pltpu.get_barrier_semaphore()
-    lines = [[tuple(o if a == d else 0 for a in range(3)) for o in range(1, sizes[d])] for d in range(3)]
-    near = lines[0] + lines[1] + lines[2]
-    for off in near:
-        pl.semaphore_signal(barrier, inc=1, device_id=at(off), device_id_type=MESH)
-
     def tell(i, line):
         for off in line:
             pl.semaphore_signal(ready.at[i], inc=1, device_id=at(off), device_id_type=MESH)
+
+    for cp in small:
+        cp.wait()
 
     row = lax.broadcasted_iota(jnp.int32, (8, L), 0)
     lane = lax.broadcasted_iota(jnp.int32, (8, L), 1)
@@ -190,14 +197,16 @@
 
         species_loop(one, 4)
 
-    def outer(k, part, fin):
-        edge = (lane < 2) | (lane >= L - 2)
+    def outer_z(k):
         for q in range(4):
             lo = zlo[k, pl.ds(8 * q, 8), :]
             hi = zhi[k, pl.ds(8 * q, 8), :]
             from_hi = mz1 * (16.0 * f(pp == 1) * pltpu.roll(hi, L - 1, 1) - pltpu.roll(hi, L - 2, 1))
             from_lo = mz0 * (16.0 * f(pp == 2) * pltpu.roll(lo, 1, 1) - pltpu.roll(lo, 2, 1))
             zk[pl.ds(8 * q, 8), :] = jnp.where(pp < 2, from_hi, from_lo)
+
+    def outer(k, h, part, fin):
+        edge = (lane < 2) | (lane >= L - 2)
         even = 16.0 * my0 * f(lax.rem(row, 2) == 0)
         odd = 16.0 * my1 * f(lax.rem(row, 2) == 1)
         lo16, hi16, dr = 16.0 * mx0 * low_rows, 16.0 * mx1 * high_rows, DRIFT * mx0 * low_rows
@@ -206,17 +215,19 @@
             zt = zk[tile8(i), :]
             for g, s in enumerate(species):
                 c = diff_ref[s] * (1.0 / 12.0)
-                xl, xh = xlo[k, s], xhi[k, s]
                 a, b = yra[k, s], yrb[k, s]
-                rl, rh = pltpu.roll(xl, 4, 0), pltpu.roll(xh, 4, 0)
                 ca = even * pltpu.roll(a, 7, 0) - my0 * a
                 cb = odd * pltpu.roll(b, 1, 0) - my1 * b
-                z0 = pltpu.roll(zt, (2 * L - 2 - 8 * g) % L, 1)
-                z1 = pltpu.roll(zt, (2 * L - 6 - 8 * g) % L, 1)
-                l0 = lo16 * rl - mx0 * xl + jnp.where(yy < 2, ca, pltpu.roll(cb, 2, 0)) + jnp.where(edge, z0, 0.0)
-                l1 = hi16 * rh - mx1 * xh + jnp.where(yy < 2, pltpu.roll(ca, 6, 0), cb) + jnp.where(edge, z1, 0.0)
-                fin(s, 0, rd(part, s, 0) + c * l0 + dr * rl)
-                fin(s, 1, rd(part, s, 1) + c * l1)
+                z = jnp.where(edge, pltpu.roll(zt, (2 * L - 2 - 8 * g - 4 * h) % L, 1), 0.0)
+                if h == 0:
+                    x = xlo[k, s]
+                    turned = pltpu.roll(x, 4, 0)
+                    lap = lo16 * turned - mx0 * x + jnp.where(yy < 2, ca, pltpu.roll(cb, 2, 0)) + z
+                    fin(s, h, rd(part, s, h) + c * lap + dr * turned)
+                else:
+                    x = xhi[k, s]
+                    lap = hi16 * pltpu.roll(x, 4, 0) - mx1 * x + jnp.where(yy < 2, pltpu.roll(ca, 6, 0), cb) + z
+                    fin(s, h, rd(part, s, h) + c * lap)
 
         block_loop(some)
 
@@ -232,9 +243,9 @@
             start = pl.multiple_of(start, 8)
         return cbuf[pl.ds(start, 8), :]
 
-    def chemistry():
+    def chemistry(first=0, rows_done=R):
         lhs = rows_lhs()
-        for r in range(0, R, 2):
+        for r in range(first, first + rows_done, 2):
             t = jnp.concatenate([tbuf[pl.ds(r + i, SP, stride=R), :] for i in range(2)], axis=1)
             hi = t.astype(jnp.bfloat16)
             lo = (t - hi.astype(jnp.float32)).astype(jnp.bfloat16)
@@ -248,33 +259,34 @@
         lo = (both - hi.astype(jnp.float32)).astype(jnp.bfloat16)
         return jnp.concatenate([hi, lo], axis=1)
 
-    def matvec():
+    def matvec(h, total):
         last = S - GROUP
         steps = -(-S // GROUP)
         again = steps * GROUP - S
+        hs = pl.ds(8 * h, 8)
 
         def columns(s0, j0, count, accs):
             accs = list(accs)
             for jj in range(count):
-                g = gee[j0 + jj]
+                g = gee[j0 + jj, hs, :]
                 for k in range(GROUP):
-                    accs[k] = accs[k] + inv[s0 + k, j0 + jj] * g
+                    accs[k] = accs[k] + inv[s0 + k, j0 + jj, hs, :] * g
             return tuple(accs)
 
         def body(i, total):
             s0 = jnp.minimum(i * GROUP, last)
-            accs = tuple(jnp.zeros((R, L), jnp.float32) for _ in range(GROUP))
+            accs = tuple(jnp.zeros((8, L), jnp.float32) for _ in range(GROUP))
             accs = lax.fori_loop(0, S // JB, lambda t, acc: columns(s0, t * JB, JB, acc), accs)
             accs = columns(s0, S // JB * JB, S % JB, accs)
             fresh = jnp.where(i == steps - 1, 0.0, 1.0)
             for k in range(GROUP):
-                dee[s0 + k] = accs[k]
-                u = accs[k] * wts[s0 + k]
+                dee[s0 + k, hs, :] = accs[k]
+                u = accs[k] * wts[s0 + k, hs, :]
                 u = u * u
                 total = total + (u * fresh if k < again else u)
             return total
 
-        return lax.fori_loop(0, steps, body, jnp.zeros((R, L), jnp.float32))
+        return lax.fori_loop(0, steps, body, total)
 
     def damping(k, total):
         rows[k, pl.ds(me, 1), :] = jnp.sum(total, axis=0, keepdims=True)
@@ -296,18 +308,20 @@
 
     halves = [(0, pl.ds(0, 8)), (1, pl.ds(8, 8))]
 
-    def newton(k, last):
-        chemistry()
-
-        def first(s):
-            for h, hs in halves:
+    def newton(k, last, faces):
+        total = jnp.zeros((8, L), jnp.float32)
+        for h, hs in halves:
+            faces(h)
+            chemistry(8 * h, 8)
+
+            def first(s):
                 gee[s, hs, :] = -GAMMA * chem_at(s, h)
 
-        species_loop(first)
-        if k == 0:
-            for cp in inv_loads:
-                cp.wait()
-        total = matvec()
+            species_loop(first)
+            if k == 0 and h == 0:
+                for cp in inv_loads:
+                    cp.wait()
+            total = matvec(h, total)
         if k == 0:
             pl.semaphore_wait(ready.at[1], len(lines[0]))
         r = damping(k, total)
@@ -326,7 +340,7 @@
                 gee[s, hs, :] = zed[s, hs, :] - base[s, hs, :] - GAMMA * chem_at(s, h)
 
         species_loop(second)
-        r2 = damping(k + 1, matvec())
+        r2 = damping(k + 1, matvec(1, matvec(0, jnp.zeros((8, L), jnp.float32))))
 
         def end(s):
             for h, hs in halves:
@@ -341,7 +355,7 @@
     pack(st, 0)
     pl.semaphore_wait(barrier, len(near))
     first_halo = halo_copies(st, 0)
-    for cp in first_halo:
+    for cp in first_halo[:1] + first_halo[2:]:
         cp.start()
     tell(0, lines[1])
     inner(st, e0)
@@ -352,8 +366,8 @@
         wts[s] = 1.0 / (REL_TOL * jnp.abs(st[s]) + ABS_TOL)
 
     species_loop(weigh)
-    for cp in first_halo:
-        cp.wait_recv()
+    first_halo[0].wait_send()
+    first_halo[1].start()
 
     def fin0(s, h, e):
         hs = pl.ds(8 * h, 8)
@@ -362,17 +376,23 @@
         base[s, hs, :] = b
         put_tanh(s, h, b)
 
-    outer(0, e0, fin0)
+    def faces0(h):
+        if h == 0:
+            for cp in first_halo[:1] + first_halo[2:]:
+                cp.wait_recv()
+            outer_z(0)
+        else:
+            first_halo[1].wait_recv()
+        outer(0, h, e0, fin0)
 
     def keep(s, h, v):
         sec[s, pl.ds(8 * h, 8), :] = v
         put_tanh(s, h, v)
 
-    newton(0, keep)
+    newton(0, keep, faces0)
 
     second_halo = halo_copies(sec, 1)
-    for cp in second_halo[:2]:
-        cp.start()
+    second_halo[0].start()
     pack(sec, 1)
     for cp in second_halo[2:]:
         cp.start()
@@ -384,8 +404,8 @@
             base[s, hs, :] = st[s, hs, :] + DELTA * e0[s, hs, :] + (1.0 - GAMMA) * chem_at(s, h)
 
     species_loop(pre)
-    for cp in second_halo:
-        cp.wait_recv()
+    second_halo[0].wait_send()
+    second_halo[1].start()
 
     def fin1(s, h, e):
         hs = pl.ds(8 * h, 8)
@@ -393,13 +413,20 @@
         base[s, hs, :] = b
         put_tanh(s, h, b)
 
-    outer(1, ebuf, fin1)
+    def faces1(h):
+        if h == 0:
+            for cp in second_halo[:1] + second_halo[2:]:
+                cp.wait_recv()
+            outer_z(1)
+        else:
+            second_halo[1].wait_recv()
+        outer(1, h, ebuf, fin1)
 
     def give(s, h, v):
         out_ref[s, pl.ds(8 * h, 8), :] = v
 
-    newton(2, give)
-    for cp in first_halo + second_halo:
+    newton(2, give, faces1)
+    for cp in first_halo[1:] + second_halo[1:]:
         cp.wait_send()
     for k in range(4):
         all_rows(k).wait_send()
@@ -415,14 +442,11 @@
         name="ark_step",
         out_shape=jax.ShapeDtypeStruct((S, R, L), jnp.float32),
         in_specs=[
-            pl.BlockSpec(memory_space=pl.ANY),
-            pl.BlockSpec(memory_space=pltpu.SMEM),
-            pl.BlockSpec(memory_space=pltpu.VMEM),
-            pl.BlockSpec(memory_space=pl.ANY),
-            pl.BlockSpec(memory_space=pltpu.SMEM),
+            pl.BlockSpec(memory_space=pltpu.HBM) for _ in range(5)
         ],
         out_specs=pl.BlockSpec(memory_space=pltpu.VMEM),
         scratch_shapes=[
+            pltpu.SMEM((S,), jnp.float32), pltpu.VMEM((S, S), jnp.float32), pltpu.SMEM((3,), jnp.int32),
             field, pltpu.VMEM((S, S, R, L), jnp.float32),
             faces, faces, faces, faces, faces, faces,
             pltpu.VMEM((2, 32, L), jnp.float32), pltpu.VMEM((32, L), jnp.float32),
@@ -430,13 +454,14 @@
             field, field, field, field, field, field, field, field,
             pltpu.VMEM((SP * R, L), jnp.float32), pltpu.VMEM((SP * R, L), jnp.float32),
             pltpu.VMEM((SP, L), jnp.float32), pltpu.VMEM((4, n_all, L), jnp.float32),
-            pltpu.SemaphoreType.DMA, pltpu.SemaphoreType.DMA((CHUNKS,)),
+            pltpu.SemaphoreType.DMA((4,)), pltpu.SemaphoreType.DMA((CHUNKS,)),
             pltpu.SemaphoreType.DMA((2, 6)), pltpu.SemaphoreType.DMA((2, 6)),
             pltpu.SemaphoreType.DMA((4,)), pltpu.SemaphoreType.DMA((4,)), pltpu.SemaphoreType.REGULAR((2,)),
         ],
-        compiler_params=pltpu.CompilerParams(collective_id=0, has_side_effects=True),
+        compiler_params=pltpu.CompilerParams(collective_id=0, has_side_effects=True, vmem_limit_bytes=48 << 20),
     )(
-        state.reshape(S, R, L), diffusivity, rates, inverse.reshape(S, S, R, L), boundary,
+        *[pltpu.with_memory_space_constraint(a, pltpu.HBM) for a in (
+            state.reshape(S, R, L), diffusivity, rates, inverse.reshape(S, S, R, L), boundary)],
     )
     return out.reshape(shape)
 

time: 75.9 us -> 70.4 us (0.928)
  Pallas kernels: 73.9 us -> 69.5 us
  local copies, waits for them, and re-layouts: 1.8 us -> 0.76 us
    pallas_call x1, Pallas kernels: 73.9 us -> 69.5 us  [body(): pl.pallas_call(functools.partial(kernel, sizes), name='ark_step', out_sha...]
    unnamed x1, local copies, waits for them, and re-layouts: 1.8 us -> 0.76 us
where the time goes in v3:
time: 70.4 us; the launch traced here: 70.3 us
  Pallas kernels  69.5 us (99%)
  local copies, waits for them, and re-layouts  0.76 us (1%)
    pallas_call x1, Pallas kernels, body(): pl.pallas_call(functools.partial(kernel, sizes), name='ark_step', out_sha...  69.5 us

profile of v3, /device:TPU:1, one launch (start us, length us, event | category | flops | bytes accessed | tf_op | source)
XLA Modules:
  0.0 70.3 jit_solution(5881851771698555001)
XLA Ops:
  0.0 69.5 %ark_step.1 = f32[53,16,128]{2,1,0:T(8,128)S(1)} custom-call(f32[53,16,128]{2,1,0:T(8,128)} %bitcast.5, f32[53]{0:T(128)} %diff_hbm.1, f32[53,53]{1,0:T(8,128)} %rates_hbm.1, f32[53,53,16,128]{3,2,1,0:T(8,128)} %bitcast.4, s32[3]{0:T(128)} %bound_hbm.1), custom_call_target="tpu_custom_call" | custom-call | tf_op jit(solution)/shard_map/ark_step/pallas_call | solution.py:440
  69.5 0.8 %copy.7 = f32[53,4,4,128]{3,2,1,0:T(4,128)} copy(f32[53,4,4,128]{3,2,1,0:T(4,128)S(1)} %bitcast.3) | data formatting | bytes 868352

commit v4 on v3

--- a/solution.py
+++ b/solution.py
@@ -23,6 +23,7 @@
 L = 128
 GROUP = 18
 JB = 8
+EARLY = 17
 CHUNKS = 8
 
 
@@ -43,7 +44,7 @@
     return sorted(out, key=lambda off: -hops(off))
 
 
-def species_loop(fn, block=4):
+def species_loop(fn, block=8):
     whole = S // block
 
     def body(i, carry):
@@ -56,8 +57,12 @@
         fn(s)
 
 
-def block_loop(fn, block=16):
+def block_loop(fn, block=16, unroll=False):
     whole = S // block
+    if unroll:
+        for i in range(whole + 1):
+            fn(i, list(range(i * block, min(S, (i + 1) * block))))
+        return
 
     def body(i, carry):
         fn(i, [i * block + k for k in range(block)])
@@ -75,9 +80,9 @@
     sizes,
     state_hbm, diff_hbm, rates_hbm, inv_hbm, bound_hbm,
     out_ref,
-    diff_ref, rates_ref, bound_ref, st, inv, xlo, xhi, ya, yb, yra, yrb, zp, zk, zlo, zhi,
-    e0, ebuf, wts, base, zed, sec, dee, gee, tbuf, cbuf, rpad, rows,
-    load_sem, inv_sem, halo_send, halo_recv, norm_send, norm_recv, ready,
+    diff_ref, rates_ref, bound_ref, st, inv, xlo, xhi, dlo, dhi, ya, yb, yra, yrb, zp, zk, zlo, zhi,
+    e0, ebuf, wts, base, zed, sec, dee, tbuf, cbuf, rpad, rows,
+    load_sem, inv_sem, halo_send, halo_recv, early_send, early_recv, norm_send, norm_recv, ready,
 ):
     n_all = sizes[0] * sizes[1] * sizes[2]
     entries = float(S * R * L * n_all)
@@ -89,10 +94,13 @@
 
     peers = offsets(sizes)
 
+    ahead = [(1, 0, 0), (0, 1, 0), (0, 0, 1)]
+    back = [tuple((sizes[d] - 1) * o for d, o in enumerate(off)) for off in ahead]
+
     barrier = pltpu.get_barrier_semaphore()
     lines = [[tuple(o if a == d else 0 for a in range(3)) for o in range(1, sizes[d])] for d in range(3)]
     near = lines[0] + lines[1] + lines[2]
-    for off in near:
+    for off in ahead[:1] + back[:1] + [o for o in near if o not in (ahead[0], back[0])]:
         pl.semaphore_signal(barrier, inc=1, device_id=at(off), device_id_type=MESH)
 
     load = pltpu.make_async_copy(state_hbm, st, load_sem.at[0])
@@ -149,21 +157,27 @@
 
         block_loop(some)
 
-    def halo_copies(field, k):
-        nx, ny, nz = sizes
+    def remote(src, dst, off, send, recv):
+        return pltpu.make_async_remote_copy(
+            src_ref=src, dst_ref=dst, send_sem=send, recv_sem=recv, device_id=at(off), device_id_type=MESH)
+
+    def x_pair(field, first, count, lo, hi, sends, recvs, i):
+        some = pl.ds(first, count)
+        return [
+            remote(field.at[some, pl.ds(8, 8), :], lo.at[some], ahead[0], sends.at[i], recvs.at[i]),
+            remote(field.at[some, pl.ds(0, 8), :], hi.at[some], back[0], sends.at[i + 1], recvs.at[i + 1]),
+        ]
+
+    def halo_copies(field, k, first):
         todo = [
-            (field.at[:, pl.ds(8, 8), :], xlo.at[k], (1, 0, 0)),
-            (field.at[:, pl.ds(0, 8), :], xhi.at[k], (nx - 1, 0, 0)),
-            (zp.at[k], zlo.at[k], (0, 0, 1)),
-            (zp.at[k], zhi.at[k], (0, 0, nz - 1)),
-            (ya.at[k], yra.at[k], (0, 1, 0)),
-            (yb.at[k], yrb.at[k], (0, ny - 1, 0)),
+            (zp.at[k], zlo.at[k], ahead[2]),
+            (zp.at[k], zhi.at[k], back[2]),
+            (ya.at[k], yra.at[k], ahead[1]),
+            (yb.at[k], yrb.at[k], back[1]),
         ]
-        cps = []
-        for i, (src, dst, off) in enumerate(todo):
-            cps.append(pltpu.make_async_remote_copy(
-                src_ref=src, dst_ref=dst, send_sem=halo_send.at[k, i], recv_sem=halo_recv.at[k, i],
-                device_id=at(off), device_id_type=MESH))
+        cps = x_pair(field, first, S - first, xlo.at[k], xhi.at[k], halo_send.at[k], halo_recv.at[k], 0)
+        for i, (src, dst, off) in enumerate(todo, 2):
+            cps.append(remote(src, dst, off, halo_send.at[k, i], halo_recv.at[k, i]))
         return cps
 
     def inner(field, out):
@@ -205,7 +219,7 @@
             from_lo = mz0 * (16.0 * f(pp == 2) * pltpu.roll(lo, 1, 1) - pltpu.roll(lo, 2, 1))
             zk[pl.ds(8 * q, 8), :] = jnp.where(pp < 2, from_hi, from_lo)
 
-    def outer(k, h, part, fin):
+    def outer(k, h, part, fin, r=None):
         edge = (lane < 2) | (lane >= L - 2)
         even = 16.0 * my0 * f(lax.rem(row, 2) == 0)
         odd = 16.0 * my1 * f(lax.rem(row, 2) == 1)
@@ -221,27 +235,26 @@
                 z = jnp.where(edge, pltpu.roll(zt, (2 * L - 2 - 8 * g - 4 * h) % L, 1), 0.0)
                 if h == 0:
                     x = xlo[k, s]
+                    if r is not None and s < EARLY:
+                        x = x - dlo[s] * r
                     turned = pltpu.roll(x, 4, 0)
                     lap = lo16 * turned - mx0 * x + jnp.where(yy < 2, ca, pltpu.roll(cb, 2, 0)) + z
                     fin(s, h, rd(part, s, h) + c * lap + dr * turned)
                 else:
                     x = xhi[k, s]
+                    if r is not None and s < EARLY:
+                        x = x - dhi[s] * r
                     lap = hi16 * pltpu.roll(x, 4, 0) - mx1 * x + jnp.where(yy < 2, pltpu.roll(ca, 6, 0), cb) + z
                     fin(s, h, rd(part, s, h) + c * lap)
 
-        block_loop(some)
+        block_loop(some, unroll=r is not None)
+
+    def cell_rows(s, h):
+        start = s * R + 8 * h
+        return pl.ds(start if isinstance(start, int) else pl.multiple_of(start, 8), 8)
 
     def put_tanh(s, h, v):
-        start = s * R + 8 * h
-        if not isinstance(s, int):
-            start = pl.multiple_of(start, 8)
-        tbuf[pl.ds(start, 8), :] = jnp.tanh(v)
-
-    def chem_at(s, h):
-        start = s * R + 8 * h
-        if not isinstance(s, int):
-            start = pl.multiple_of(start, 8)
-        return cbuf[pl.ds(start, 8), :]
+        tbuf[cell_rows(s, h), :] = jnp.tanh(v)
 
     def chemistry(first=0, rows_done=R):
         lhs = rows_lhs()
@@ -268,7 +281,7 @@
         def columns(s0, j0, count, accs):
             accs = list(accs)
             for jj in range(count):
-                g = gee[j0 + jj, hs, :]
+                g = cbuf[cell_rows(j0 + jj, h), :]
                 for k in range(GROUP):
                     accs[k] = accs[k] + inv[s0 + k, j0 + jj, hs, :] * g
             return tuple(accs)
@@ -288,13 +301,15 @@
 
         return lax.fori_loop(0, steps, body, total)
 
-    def damping(k, total):
+    def share(k, total):
         rows[k, pl.ds(me, 1), :] = jnp.sum(total, axis=0, keepdims=True)
         for off in peers:
             pltpu.make_async_remote_copy(
                 src_ref=rows.at[k, pl.ds(me, 1), :], dst_ref=rows.at[k, pl.ds(me, 1), :],
                 send_sem=norm_send.at[k], recv_sem=norm_recv.at[k],
                 device_id=at(off), device_id_type=MESH).start()
+
+    def damped(k):
         all_rows(k).wait_recv()
         total = jnp.sum(jnp.sum(rows[k], axis=0, keepdims=True), axis=1, keepdims=True)
         return 1.0 / jnp.maximum(jnp.sqrt(total * (1.0 / entries)), 1.0)
@@ -308,23 +323,19 @@
 
     halves = [(0, pl.ds(0, 8)), (1, pl.ds(8, 8))]
 
-    def newton(k, last, faces):
+    def newton(k, last, faces, with_mid=None, with_update=None):
         total = jnp.zeros((8, L), jnp.float32)
         for h, hs in halves:
             faces(h)
             chemistry(8 * h, 8)
-
-            def first(s):
-                gee[s, hs, :] = -GAMMA * chem_at(s, h)
-
-            species_loop(first)
             if k == 0 and h == 0:
                 for cp in inv_loads:
                     cp.wait()
             total = matvec(h, total)
         if k == 0:
             pl.semaphore_wait(ready.at[1], len(lines[0]))
-        r = damping(k, total)
+        share(k, total)
+        r = damped(k)
 
         def mid(s):
             for h, hs in halves:
@@ -333,28 +344,34 @@
                 put_tanh(s, h, z)
 
         species_loop(mid)
+        if with_mid is not None:
+            with_mid()
         chemistry()
 
         def second(s):
             for h, hs in halves:
-                gee[s, hs, :] = zed[s, hs, :] - base[s, hs, :] - GAMMA * chem_at(s, h)
+                cbuf[cell_rows(s, h), :] += zed[s, hs, :] - base[s, hs, :]
 
         species_loop(second)
-        r2 = damping(k + 1, matvec(1, matvec(0, jnp.zeros((8, L), jnp.float32))))
+        share(k + 1, matvec(1, matvec(0, jnp.zeros((8, L), jnp.float32))))
+        if with_update is not None:
+            with_update()
+        r2 = damped(k + 1)
 
         def end(s):
             for h, hs in halves:
                 last(s, h, zed[s, hs, :] - dee[s, hs, :] * r2)
 
         species_loop(end)
+        return r2
 
     tbuf[pl.ds(S * R, (SP - S) * R), :] = jnp.zeros(((SP - S) * R, L), jnp.float32)
     rpad[...] = jnp.zeros((SP, L), jnp.float32)
-    rpad[0:S, 0:S] = rates_ref[...]
+    rpad[0:S, 0:S] = -GAMMA * rates_ref[...]
     load.wait()
     pack(st, 0)
     pl.semaphore_wait(barrier, len(near))
-    first_halo = halo_copies(st, 0)
+    first_halo = halo_copies(st, 0, 0)
     for cp in first_halo[:1] + first_halo[2:]:
         cp.start()
     tell(0, lines[1])
@@ -389,9 +406,20 @@
         sec[s, pl.ds(8 * h, 8), :] = v
         put_tanh(s, h, v)
 
-    newton(0, keep, faces0)
-
-    second_halo = halo_copies(sec, 1)
+    early = (x_pair(zed, 0, EARLY, xlo.at[1], xhi.at[1], early_send, early_recv, 0)
+             + x_pair(dee, 0, EARLY, dlo, dhi, early_send, early_recv, 2))
+
+    def with_mid():
+        for cp in early[:2]:
+            cp.start()
+
+    def with_update():
+        for cp in early[2:]:
+            cp.start()
+
+    r2 = newton(0, keep, faces0, with_mid, with_update)
+
+    second_halo = halo_copies(sec, 1, EARLY)
     second_halo[0].start()
     pack(sec, 1)
     for cp in second_halo[2:]:
@@ -401,9 +429,11 @@
 
     def pre(s):
         for h, hs in halves:
-            base[s, hs, :] = st[s, hs, :] + DELTA * e0[s, hs, :] + (1.0 - GAMMA) * chem_at(s, h)
+            base[s, hs, :] = st[s, hs, :] + DELTA * e0[s, hs, :] + (1.0 - 1.0 / GAMMA) * cbuf[cell_rows(s, h), :]
 
     species_loop(pre)
+    for cp in early:
+        cp.wait()
     second_halo[0].wait_send()
     second_halo[1].start()
 
@@ -420,7 +450,7 @@
             outer_z(1)
         else:
             second_halo[1].wait_recv()
-        outer(1, h, ebuf, fin1)
+        outer(1, h, ebuf, fin1, r2)
 
     def give(s, h, v):
         out_ref[s, pl.ds(8 * h, 8), :] = v
@@ -436,6 +466,7 @@
     shape = state.shape
     field = pltpu.VMEM((S, R, L), jnp.float32)
     faces = pltpu.VMEM((2, S, 8, L), jnp.float32)
+    early = pltpu.VMEM((EARLY, 8, L), jnp.float32)
     n_all = sizes[0] * sizes[1] * sizes[2]
     out = pl.pallas_call(
         functools.partial(kernel, sizes),
@@ -448,14 +479,15 @@
         scratch_shapes=[
             pltpu.SMEM((S,), jnp.float32), pltpu.VMEM((S, S), jnp.float32), pltpu.SMEM((3,), jnp.int32),
             field, pltpu.VMEM((S, S, R, L), jnp.float32),
-            faces, faces, faces, faces, faces, faces,
+            faces, faces, early, early, faces, faces, faces, faces,
             pltpu.VMEM((2, 32, L), jnp.float32), pltpu.VMEM((32, L), jnp.float32),
             pltpu.VMEM((2, 32, L), jnp.float32), pltpu.VMEM((2, 32, L), jnp.float32),
-            field, field, field, field, field, field, field, field,
+            field, field, field, field, field, field, field,
             pltpu.VMEM((SP * R, L), jnp.float32), pltpu.VMEM((SP * R, L), jnp.float32),
             pltpu.VMEM((SP, L), jnp.float32), pltpu.VMEM((4, n_all, L), jnp.float32),
             pltpu.SemaphoreType.DMA((4,)), pltpu.SemaphoreType.DMA((CHUNKS,)),
             pltpu.SemaphoreType.DMA((2, 6)), pltpu.SemaphoreType.DMA((2, 6)),
+            pltpu.SemaphoreType.DMA((4,)), pltpu.SemaphoreType.DMA((4,)),
             pltpu.SemaphoreType.DMA((4,)), pltpu.SemaphoreType.DMA((4,)), pltpu.SemaphoreType.REGULAR((2,)),
         ],
         compiler_params=pltpu.CompilerParams(collective_id=0, has_side_effects=True, vmem_limit_bytes=48 << 20),

time: 70.4 us -> 67.5 us (0.959)
  Pallas kernels: 69.5 us -> 66.6 us
    pallas_call x1, Pallas kernels: 69.5 us -> 66.6 us  [body(): pl.pallas_call(functools.partial(kernel, sizes), name='ark_step', out_sha...]
where the time goes in v4:
time: 67.5 us; the launch traced here: 67.4 us
  Pallas kernels  66.6 us (99%)
  local copies, waits for them, and re-layouts  0.76 us (1%)
    pallas_call x1, Pallas kernels, body(): pl.pallas_call(functools.partial(kernel, sizes), name='ark_step', out_sha...  66.6 us

profile of v4, /device:TPU:1, one launch (start us, length us, event | category | flops | bytes accessed | tf_op | source)
XLA Modules:
  0.0 67.4 jit_solution(9421912745014805308)
XLA Ops:
  0.0 66.6 %ark_step.1 = f32[53,16,128]{2,1,0:T(8,128)S(1)} custom-call(f32[53,16,128]{2,1,0:T(8,128)} %bitcast.5, f32[53]{0:T(128)} %diff_hbm.1, f32[53,53]{1,0:T(8,128)} %rates_hbm.1, f32[53,53,16,128]{3,2,1,0:T(8,128)} %bitcast.4, s32[3]{0:T(128)} %bound_hbm.1), custom_call_target="tpu_custom_call" | custom-call | tf_op jit(solution)/shard_map/ark_step/pallas_call | solution.py:471
  66.6 0.8 %copy.7 = f32[53,4,4,128]{3,2,1,0:T(4,128)} copy(f32[53,4,4,128]{3,2,1,0:T(4,128)S(1)} %bitcast.3) | data formatting | bytes 868352

commit v5 on v4

--- a/solution.py
+++ b/solution.py
@@ -22,7 +22,7 @@
 R = 16
 L = 128
 GROUP = 18
-JB = 8
+JB = 13
 EARLY = 17
 CHUNKS = 8
 
@@ -376,8 +376,6 @@
         cp.start()
     tell(0, lines[1])
     inner(st, e0)
-    pl.semaphore_wait(ready.at[0], len(lines[1]))
-    tell(1, lines[0])
 
     def weigh(s):
         wts[s] = 1.0 / (REL_TOL * jnp.abs(st[s]) + ABS_TOL)
@@ -385,6 +383,8 @@
     species_loop(weigh)
     first_halo[0].wait_send()
     first_halo[1].start()
+    pl.semaphore_wait(ready.at[0], len(lines[1]))
+    tell(1, lines[0])
 
     def fin0(s, h, e):
         hs = pl.ds(8 * h, 8)
@@ -404,7 +404,6 @@
 
     def keep(s, h, v):
         sec[s, pl.ds(8 * h, 8), :] = v
-        put_tanh(s, h, v)
 
     early = (x_pair(zed, 0, EARLY, xlo.at[1], xhi.at[1], early_send, early_recv, 0)
              + x_pair(dee, 0, EARLY, dlo, dhi, early_send, early_recv, 2))
@@ -424,6 +423,12 @@
     pack(sec, 1)
     for cp in second_halo[2:]:
         cp.start()
+
+    def section_tanh(s):
+        for h, hs in halves:
+            put_tanh(s, h, sec[s, hs, :])
+
+    species_loop(section_tanh)
     inner(sec, ebuf)
     chemistry()
 

time: 67.5 us -> 67 us (level)
  no operation moved by 1% of the time
where the time goes in v5:
time: 67 us; the launch traced here: 66.9 us
  Pallas kernels  66.2 us (99%)
  local copies, waits for them, and re-layouts  0.76 us (1%)
    pallas_call x1, Pallas kernels, body(): pl.pallas_call(functools.partial(kernel, sizes), name='ark_step', out_sha...  66.2 us

profile of v5, /device:TPU:1, one launch (start us, length us, event | category | flops | bytes accessed | tf_op | source)
XLA Modules:
  0.0 66.9 jit_solution(1736153022780458615)
XLA Ops:
  0.0 66.2 %ark_step.1 = f32[53,16,128]{2,1,0:T(8,128)S(1)} custom-call(f32[53,16,128]{2,1,0:T(8,128)} %bitcast.5, f32[53]{0:T(128)} %diff_hbm.1, f32[53,53]{1,0:T(8,128)} %rates_hbm.1, f32[53,53,16,128]{3,2,1,0:T(8,128)} %bitcast.4, s32[3]{0:T(128)} %bound_hbm.1), custom_call_target="tpu_custom_call" | custom-call | tf_op jit(solution)/shard_map/ark_step/pallas_call | solution.py:476
  66.2 0.8 %copy.7 = f32[53,4,4,128]{3,2,1,0:T(4,128)} copy(f32[53,4,4,128]{3,2,1,0:T(4,128)S(1)} %bitcast.3) | data formatting | bytes 868352
